TPU v7x, 32 devices: a whole 2x2x4 slice. The times are simulated.
32 devices in a mesh: dp: 2 (over y), row: 4 (over z), col: 4 (over x, core).
Axes of the slice: x: 2, y: 2, z: 4, core: 2. Of those that a mesh axis runs over, the one named last changes fastest.
Arguments:
- block_input: bfloat16 [1024, 1024], P(('dp', 'col'), 'row'), may hold values from -6 to 6
- attn_gain: float32 [1024], P('row'), may hold values from 0.25 to 1.75
- w_qkv: bfloat16 [1024, 2048], P('row', 'col'), may hold values from -0.1875 to 0.1875
- w_out: bfloat16 [1024, 1024], P('col', 'row'), may hold values from -0.75 to 0.75
- ffn_gain: float32 [1024], P('row'), may hold values from 0.25 to 1.75
- w_router: float32 [1024, 32], P('row'), may hold values from -0.0625 to 0.0625
- w_gate: bfloat16 [32, 1024, 512], P(None, 'row', 'col'), may hold values from -0.1875 to 0.1875
- w_up: bfloat16 [32, 1024, 512], P(None, 'row', 'col'), may hold values from -0.1875 to 0.1875
- w_down: bfloat16 [32, 512, 1024], P(None, 'col', 'row'), may hold values from -0.25 to 0.25
- routes: int32 [1024, 8], P('dp'), may hold values from 0 to 31, all different within a row; in each aligned block of 512 rows (0 to 511, 512 to 1023, ...) at most 192 rows name the same one
- out_grad: bfloat16 [1024, 1024], P(('dp', 'col'), 'row'), may hold values from -6 to 6
Outputs:
- block_output: bfloat16 [1024, 1024], P(('dp', 'col'), 'row')
- input_grad: float32 [1024, 1024], P(('dp', 'col'), 'row')
- grad_attn_gain: float32 [1024], P('row')
- grad_qkv: float32 [1024, 2048], P('row', 'col')
- grad_out: float32 [1024, 1024], P('col', 'row')
- grad_ffn_gain: float32 [1024], P('row')
- grad_router: float32 [1024, 32], P('row')
- grad_gate: float32 [32, 1024, 512], P('dp', 'row', 'col')
- grad_up: float32 [32, 1024, 512], P('dp', 'row', 'col')
- grad_down: float32 [32, 512, 1024], P('dp', 'col', 'row')
Inputs may be any that keep to these rules, and one draw needn't show every extreme that they name: `routes`: every row names 8 different experts. Among the 512 rows of one sequence no expert is named more than 192 times, a bound that some block reaches.
All inputs are finite; a program needn't handle non-finite values.
Results may differ from a plain program's by a relative error of at most 0.013.
Values may be sent and summed in bfloat16 or wider, within the bound.
A program may use at most 128 MiB of HBM per device.

v0:
```python
import jax
import jax.numpy as jnp
from jax import lax
from jax.sharding import PartitionSpec as P

HEADS = 16
KV_HEADS = 8
HEAD_DIM = 64
CAP = 192


epsilon = 1e-06
rope_base = 10000.0


def rotate_half(head_values):
    half_width = head_values.shape[-1] // 2
    return jnp.concatenate([-head_values[..., half_width:], head_values[..., :half_width]], axis=-1)


def rope_tables(positions, head_dim):
    half_width = head_dim // 2
    inverse = rope_base ** (-jnp.arange(half_width, dtype=jnp.float32) / half_width)
    angles = positions.astype(jnp.float32)[:, None] * inverse[None, :]
    cos_table = jnp.cos(angles)
    sin_table = jnp.sin(angles)
    return (
        jnp.concatenate([cos_table, cos_table], axis=-1),
        jnp.concatenate([sin_table, sin_table], axis=-1),
    )


def slot_tables(routes_seq, experts, capacity):
    flat_routes = routes_seq.reshape(-1)
    pair_count = flat_routes.shape[0]
    onehot = (flat_routes[:, None] == jnp.arange(experts, dtype=jnp.int32)[None, :]).astype(
        jnp.int32
    )
    before = jnp.cumsum(onehot, axis=0) - onehot
    rank_in_expert = jnp.sum(before * onehot, axis=1)
    slot_of_pair = flat_routes * capacity + rank_in_expert
    pair_of_slot = (
        jnp.zeros((experts * capacity,), jnp.int32)
        .at[slot_of_pair]
        .set(jnp.arange(pair_count, dtype=jnp.int32))
    )
    filled = jnp.zeros((experts * capacity,), jnp.int32).at[slot_of_pair].set(1)
    return (slot_of_pair, pair_of_slot, filled)


def col_rows(block_array):
    return lax.all_gather(block_array, "col", axis=0, tiled=True)


def row_rows(block_array):
    return lax.all_gather(block_array, "row", axis=0, tiled=True)


def row_terms(term_maker, local_rows):
    return lax.psum_scatter(
        term_maker(jnp.int32(0), local_rows * lax.axis_size("row")),
        "row",
        scatter_dimension=0,
        tiled=True,
    )


def col_terms(term_maker, local_rows):
    return lax.psum_scatter(
        term_maker(jnp.int32(0), local_rows * lax.axis_size("col")),
        "col",
        scatter_dimension=0,
        tiled=True,
    )


def row_total(partial_sum):
    return lax.psum(partial_sum, "row")


def slicer(full_array):

    def take_rows(first_row, row_count):
        return full_array

    return take_rows


def per_device(
    block_input, attn_gain, w_qkv, w_out, ffn_gain, w_router, w_gate, w_up, w_down, routes, out_grad
):
    tok_local, width_local = block_input.shape
    model_width = width_local * lax.axis_size("row")
    seq_len = routes.shape[0]
    top_count = routes.shape[1]
    experts = w_gate.shape[0]
    ffn_local = w_gate.shape[2]
    capacity = CAP
    repeat = HEADS // KV_HEADS
    groups_local = KV_HEADS // lax.axis_size("col")
    kv_cols = groups_local * HEAD_DIM
    query_len = seq_len // lax.axis_size("row")
    slots_local = experts * capacity // lax.axis_size("row")
    row_index = lax.axis_index("row")
    col_index = lax.axis_index("col")
    score_scale = HEAD_DIM ** (-0.5)
    inputs_f = block_input.astype(jnp.float32)
    square_one = row_total(jnp.sum(inputs_f * inputs_f, axis=1))
    inv_rms_one = lax.rsqrt(square_one / model_width + epsilon)[:, None]
    unit_one = inputs_f * inv_rms_one
    normed_one = (unit_one * attn_gain).astype(jnp.bfloat16)
    normed_all = col_rows(normed_one)

    def qkv_term(first_row, row_count):
        return jnp.dot(normed_all, w_qkv, preferred_element_type=jnp.float32)

    proj_qkv = row_terms(qkv_term, query_len).reshape(query_len, groups_local, repeat + 2, HEAD_DIM)
    positions = row_index * query_len + jnp.arange(query_len, dtype=jnp.int32)
    cos_table, sin_table = rope_tables(positions, HEAD_DIM)
    queries = proj_qkv[:, :, :repeat]
    keys_raw = proj_qkv[:, :, repeat]
    vals_raw = proj_qkv[:, :, repeat + 1]
    queries_rot = (
        (queries * cos_table[:, None, None] + rotate_half(queries) * sin_table[:, None, None])
        * score_scale
    ).astype(jnp.bfloat16)
    keys_rot = (keys_raw * cos_table[:, None] + rotate_half(keys_raw) * sin_table[:, None]).astype(
        jnp.bfloat16
    )
    key_value = jnp.concatenate(
        [
            keys_rot.reshape(query_len, kv_cols),
            vals_raw.astype(jnp.bfloat16).reshape(query_len, kv_cols),
        ],
        axis=1,
    )
    key_value_all = row_rows(key_value)
    keys_all = key_value_all[:, :kv_cols].reshape(seq_len, groups_local, HEAD_DIM)
    values_all = key_value_all[:, kv_cols:].reshape(seq_len, groups_local, HEAD_DIM)
    causal = jnp.arange(seq_len, dtype=jnp.int32)[None, :] <= positions[:, None]
    scores = jnp.einsum("qgrd,kgd->grqk", queries_rot, keys_all, preferred_element_type=jnp.float32)
    exp_scores = jnp.where(causal, jnp.exp(scores), 0.0)
    log_total = jnp.log(jnp.sum(exp_scores, axis=-1, keepdims=True))
    attn_probs = jnp.where(causal, jnp.exp(scores - log_total), 0.0)
    probs_b = attn_probs.astype(jnp.bfloat16)
    attended = (
        jnp.einsum("grqk,kgd->qgrd", probs_b, values_all, preferred_element_type=jnp.float32)
        .astype(jnp.bfloat16)
        .reshape(query_len, -1)
    )
    attended_all = row_rows(attended)

    def attn_term(first_row, row_count):
        return jnp.dot(attended_all, w_out, preferred_element_type=jnp.float32)

    hidden_res = inputs_f + col_terms(attn_term, tok_local)
    gained = hidden_res * ffn_gain
    square_two, router_part = lax.psum(
        (
            jnp.sum(hidden_res * hidden_res, axis=1),
            jnp.dot(gained, w_router, precision=lax.Precision.HIGHEST),
        ),
        "row",
    )
    inv_rms_two = lax.rsqrt(square_two / model_width + epsilon)[:, None]
    unit_two = hidden_res * inv_rms_two
    normed_two_f = gained * inv_rms_two
    normed_two = normed_two_f.astype(jnp.bfloat16)
    logits = router_part * inv_rms_two
    routes_local = lax.dynamic_slice_in_dim(routes, col_index * tok_local, tok_local, 0)
    chosen_mask = (
        routes_local[:, :, None] == jnp.arange(experts, dtype=jnp.int32)[None, None, :]
    ).astype(jnp.float32)
    chosen = jnp.sum(chosen_mask * logits[:, None, :], axis=2)
    exp_chosen = jnp.exp(chosen)
    gate_weights = exp_chosen / jnp.sum(exp_chosen, axis=1, keepdims=True)
    normed_two_all = col_rows(normed_two)
    slot_of_pair, pair_of_slot, filled = slot_tables(routes, experts, capacity)
    token_of_slot = pair_of_slot // top_count
    slot_rows = jnp.where(filled[:, None] > 0, normed_two_all[token_of_slot], 0)
    w_both = jnp.concatenate([w_gate, w_up], axis=2)
    row_block = slot_rows.reshape(
        slots_local * lax.axis_size("row") // capacity, capacity, width_local
    )
    pre_act = lax.psum_scatter(
        jnp.einsum("ecd,edf->ecf", row_block, w_both, preferred_element_type=jnp.float32).reshape(
            slots_local * lax.axis_size("row"), 2 * ffn_local
        ),
        "row",
        scatter_dimension=0,
        tiled=True,
    )
    gate_pre = pre_act[:, :ffn_local]
    up_val = pre_act[:, ffn_local:]
    sigmoid_gate = jax.nn.sigmoid(gate_pre)
    activated = (gate_pre * sigmoid_gate * up_val).astype(jnp.bfloat16)
    activated_all = row_rows(activated)
    down_slots = jnp.einsum(
        "ecf,efd->ecd",
        activated_all.reshape(experts, capacity, ffn_local),
        w_down,
        preferred_element_type=jnp.float32,
    ).reshape(experts * capacity, width_local)
    pair_out = down_slots[slot_of_pair]
    pair_local = col_terms(slicer(pair_out), tok_local * top_count).reshape(
        tok_local, top_count, width_local
    )
    block_output = (hidden_res + jnp.sum(gate_weights[:, :, None] * pair_local, axis=1)).astype(
        jnp.bfloat16
    )
    grad_f = out_grad.astype(jnp.float32)
    gate_grads = row_total(jnp.sum(grad_f[:, None, :] * pair_local, axis=2))
    gate_mix = gate_weights * (
        gate_grads - jnp.sum(gate_weights * gate_grads, axis=1, keepdims=True)
    )
    logit_grads = jnp.sum(gate_mix[:, :, None] * chosen_mask, axis=1)
    pair_grad = (
        (gate_weights[:, :, None] * grad_f[:, None, :])
        .astype(jnp.bfloat16)
        .reshape(tok_local * top_count, width_local)
    )
    pair_grad_all = col_rows(pair_grad)
    slot_grad = jnp.where(filled[:, None] > 0, pair_grad_all[pair_of_slot], 0)

    def act_term(first_row, row_count):
        row_block = slot_grad.reshape(row_count // capacity, capacity, width_local)
        return jnp.einsum(
            "ecd,efd->ecf", row_block, w_down, preferred_element_type=jnp.float32
        ).reshape(row_count, ffn_local)

    act_grad = row_terms(act_term, slots_local)
    gate_pre_grad = act_grad * up_val * sigmoid_gate * (1.0 + gate_pre * (1.0 - sigmoid_gate))
    up_grad = act_grad * gate_pre * sigmoid_gate
    pre_grad = jnp.concatenate([gate_pre_grad, up_grad], axis=1).astype(jnp.bfloat16)
    pre_grad_all = row_rows(pre_grad).reshape(experts, capacity, 2 * ffn_local)
    down_grad = jnp.einsum(
        "ecf,ecd->efd",
        activated_all.reshape(experts, capacity, ffn_local),
        slot_grad.reshape(experts, capacity, width_local),
        preferred_element_type=jnp.float32,
    )
    both_grad = jnp.einsum(
        "ecd,ecf->edf",
        slot_rows.reshape(experts, capacity, width_local),
        pre_grad_all,
        preferred_element_type=jnp.float32,
    )
    slot_back = jnp.einsum(
        "ecf,edf->ecd", pre_grad_all, w_both, preferred_element_type=jnp.float32
    ).reshape(experts * capacity, width_local)
    token_back = jnp.sum(slot_back[slot_of_pair].reshape(seq_len, top_count, width_local), axis=1)
    normed_grad = col_terms(slicer(token_back), tok_local)
    normed_grad = normed_grad + jnp.dot(logit_grads, w_router.T, precision=lax.Precision.HIGHEST)
    ffn_gain_part = jnp.sum(normed_grad * unit_two, axis=0)
    router_part_grad = jnp.dot(normed_two_f.T, logit_grads, precision=lax.Precision.HIGHEST)
    unit_grad_two = normed_grad * ffn_gain
    inner_two = row_total(jnp.sum(unit_grad_two * unit_two, axis=1))
    residual_grad = grad_f + inv_rms_two * (
        unit_grad_two - unit_two * (inner_two / model_width)[:, None]
    )
    residual_b = residual_grad.astype(jnp.bfloat16)
    residual_all = col_rows(residual_b)
    out_proj_grad = jnp.einsum(
        "th,td->hd", attended_all, residual_all, preferred_element_type=jnp.float32
    )

    def attn_back_term(first_row, row_count):
        return jnp.einsum("td,hd->th", residual_all, w_out, preferred_element_type=jnp.float32)

    attended_grad = (
        row_terms(attn_back_term, query_len)
        .astype(jnp.bfloat16)
        .reshape(query_len, groups_local, repeat, HEAD_DIM)
    )
    prob_grad = jnp.einsum(
        "qgrd,kgd->grqk", attended_grad, values_all, preferred_element_type=jnp.float32
    )
    prob_inner = jnp.sum(attn_probs * prob_grad, axis=-1, keepdims=True)
    score_grad = (attn_probs * (prob_grad - prob_inner)).astype(jnp.bfloat16)
    query_grad = jnp.einsum(
        "grqk,kgd->qgrd", score_grad, keys_all, preferred_element_type=jnp.float32
    )
    key_part = jnp.einsum(
        "grqk,qgrd->kgd", score_grad, queries_rot, preferred_element_type=jnp.float32
    )
    value_part = jnp.einsum(
        "grqk,qgrd->kgd", probs_b, attended_grad, preferred_element_type=jnp.float32
    )
    kv_part = jnp.concatenate(
        [key_part.reshape(seq_len, kv_cols), value_part.reshape(seq_len, kv_cols)], axis=1
    )
    kv_grad = row_terms(slicer(kv_part), query_len)
    key_grad = kv_grad[:, :kv_cols].reshape(query_len, groups_local, HEAD_DIM)
    value_grad = kv_grad[:, kv_cols:].reshape(query_len, groups_local, HEAD_DIM)
    query_back = (
        query_grad * cos_table[:, None, None] - rotate_half(query_grad * sin_table[:, None, None])
    ) * score_scale
    key_back = key_grad * cos_table[:, None] - rotate_half(key_grad * sin_table[:, None])
    qkv_grad = (
        jnp.concatenate([query_back, key_back[:, :, None], value_grad[:, :, None]], axis=2)
        .reshape(query_len, -1)
        .astype(jnp.bfloat16)
    )
    qkv_grad_all = row_rows(qkv_grad)
    qkv_weight_part = jnp.einsum(
        "td,tc->dc", normed_all, qkv_grad_all, preferred_element_type=jnp.float32
    )

    def norm_back_term(first_row, row_count):
        return jnp.einsum("tc,dc->td", qkv_grad_all, w_qkv, preferred_element_type=jnp.float32)

    normed_one_grad = col_terms(norm_back_term, tok_local)
    attn_gain_part = jnp.sum(normed_one_grad * unit_one, axis=0)
    unit_grad_one = normed_one_grad * attn_gain
    inner_one = row_total(jnp.sum(unit_grad_one * unit_one, axis=1))
    input_grad = residual_grad + inv_rms_one * (
        unit_grad_one - unit_one * (inner_one / model_width)[:, None]
    )
    grad_qkv, grad_out = (
        lax.psum(qkv_weight_part.astype(jnp.bfloat16), "dp").astype(jnp.float32),
        lax.psum(out_proj_grad.astype(jnp.bfloat16), "dp").astype(jnp.float32),
    )
    grad_attn_gain, grad_ffn_gain, grad_router = lax.psum(
        (attn_gain_part, ffn_gain_part, router_part_grad), ("dp", "col")
    )
    grad_gate, grad_up, grad_down = (
        lax.psum_scatter(
            both_grad[:, :, :ffn_local].astype(jnp.bfloat16), "dp", scatter_dimension=0, tiled=True
        ).astype(jnp.float32),
        lax.psum_scatter(
            both_grad[:, :, ffn_local:].astype(jnp.bfloat16), "dp", scatter_dimension=0, tiled=True
        ).astype(jnp.float32),
        lax.psum_scatter(
            down_grad.astype(jnp.bfloat16), "dp", scatter_dimension=0, tiled=True
        ).astype(jnp.float32),
    )
    return (
        block_output,
        input_grad,
        grad_attn_gain,
        grad_qkv,
        grad_out,
        grad_ffn_gain,
        grad_router,
        grad_gate,
        grad_up,
        grad_down,
    )


def solution(mesh):
    in_specs = (
        P(("dp", "col"), "row"),
        P("row"),
        P("row", "col"),
        P("col", "row"),
        P("row"),
        P("row", None),
        P(None, "row", "col"),
        P(None, "row", "col"),
        P(None, "col", "row"),
        P("dp", None),
        P(("dp", "col"), "row"),
    )
    out_specs = (
        P(("dp", "col"), "row"),
        P(("dp", "col"), "row"),
        P("row"),
        P("row", "col"),
        P("col", "row"),
        P("row"),
        P("row", None),
        P("dp", "row", "col"),
        P("dp", "row", "col"),
        P("dp", "col", "row"),
    )
    return jax.shard_map(
        per_device, mesh=mesh, in_specs=in_specs, out_specs=out_specs, check_vma=False
    )
```

profile of v0, /device:TPU:0, one launch (start us, length us, event | category | flops | bytes accessed | tf_op | source)
XLA Modules:
  0.0 916.7 jit_solution(3248385203202186729)
XLA Ops:
  8.3 13.5 %psum.77 = f32[128]{0:T(128)S(1)} all-reduce(f32[128]{0:T(128)S(1)} %fusion.38), channel_id=1, replica_groups=mesh['dp'=2,'row'=4,'col'=4] {'row'}, use_global_device_ids=true, to_apply=%region_1.0 | all-reduce | flops 128 | bytes 1024 | tf_op jit(solution)/shard_map/psum | solution.py:78
  58.9 13.0 %all_gather.28 = bf16[512,256]{0,1:T(8,128)(2,1)S(1)} all-gather(bf16[128,256]{0,1:T(8,128)(2,1)S(1)} %pad_maximum_fusion.3), channel_id=1, replica_groups=mesh['dp'=2,'row'=4,'col'=4] {'row'}, dimensions={0}, use_global_device_ids=true | all-gather | bytes 327680 | tf_op jit(solution)/shard_map/all_gather | solution.py:56
  91.4 15.5 %scatter_custom_fusion.1 = s32[6144]{0:T(1024)S(1)} fusion(s32[4096]{0:T(1024)S(1)} %bitcast.169, s32[4096]{0:T(1024)S(1)} %iota.33, s32[]{:T(128)} %constant.55.clone.1), kind=kCustom, calls=%fused_computation.135 | custom fusion | bytes 24580 | tf_op jit(solution)/shard_map/scatter | solution.py:45
  106.9 15.5 %scatter_custom_fusion = s32[6144]{0:T(1024)S(1)} fusion(s32[4096]{0:T(1024)S(1)} %bitcast.170, s32[4096]{0:T(1024)S(1)} %broadcast.148, s32[]{:T(128)} %constant.55.clone.1), kind=kCustom, calls=%fused_computation.138 | custom fusion | bytes 24580 | tf_op jit(solution)/shard_map/scatter | solution.py:47
  144.1 26.9 %gather_fusion = bf16[6144,256]{1,0:T(8,128)(2,1)} fusion(bf16[512,256]{1,0:T(8,128)(2,1)S(1)} %all_gather.30, s32[6144]{0:T(1024)} %get-tuple-element.44), kind=kCustom, calls=%fused_computation | custom fusion | bytes 6316032 | tf_op jit(solution)/shard_map/gather | solution.py:180
  177.3 110.5 %reduce-scatter.17.cloned.1.call-done = f32[1536,256]{1,0:T(8,128)} async-done(((f32[6144,256]{1,0:T(8,128)}), f32[1536,256]{1,0:T(8,128)}) %reduce-scatter.17.cloned.1.call-update) | async-done | bytes 1572880 | tf_op jit(solution)/shard_map/reduce_scatter | solution.py:185
  290.3 37.6 %all-gather.4.cloned.1.call-done = bf16[6144,128]{1,0:T(8,128)(2,1)} async-done(((bf16[1536,128]{1,0:T(8,128)(2,1)}), bf16[6144,128]{1,0:T(8,128)(2,1)}) %all-gather.4.cloned.1.call-update) | async-done | bytes 1572880 | tf_op jit(solution)/shard_map/all_gather | solution.py:56
  332.9 18.9 %gather_fusion.1 = f32[4096,256]{1,0:T(8,128)} fusion(f32[6144,256]{1,0:T(8,128)} %bitcast.136, s32[4096]{0:T(1024)S(1)} %broadcast_clamp_fusion), kind=kCustom, calls=%fused_computation.1 | custom fusion | bytes 8404992 | tf_op jit(solution)/shard_map/gather | solution.py:204
  354.8 40.6 %reduce-scatter.19.cloned.1.call-done = f32[1024,256]{1,0:T(8,128)} async-done(((f32[4096,256]{1,0:T(8,128)}), f32[1024,256]{1,0:T(8,128)}) %reduce-scatter.19.cloned.1.call-update) | async-done | bytes 1048592 | tf_op jit(solution)/shard_map/reduce_scatter | solution.py:69
  398.9 19.7 %all-reduce.1 = (f32[128,32]{0,1:T(8,128)S(1)}, f32[128,8]{0,1:T(8,128)S(1)}) all-reduce(f32[128,32]{0,1:T(8,128)} %fusion.47, f32[128,8]{0,1:T(8,128)} %copy.56), channel_id=1, replica_groups=mesh['dp'=2,'row'=4,'col'=4] {'row'}, use_global_device_ids=true, to_apply=%region_5.6 | all-reduce | flops 5120 | bytes 40960 | tf_op jit(solution)/shard_map/psum | solution.py:158
  424.5 19.8 %all-gather.6.cloned.1.call-done = bf16[4096,256]{1,0:T(8,128)(2,1)} async-done(((bf16[1024,256]{1,0:T(8,128)(2,1)}), bf16[4096,256]{1,0:T(8,128)(2,1)}) %all-gather.6.cloned.1.call-update) | async-done | bytes 2097168 | tf_op jit(solution)/shard_map/all_gather | solution.py:52
  444.3 27.4 %gather_fusion.2 = bf16[6144,256]{1,0:T(8,128)(2,1)} fusion(bf16[4096,256]{1,0:T(8,128)(2,1)} %all-gather.6.cloned.1.call-done, s32[6144]{0:T(1024)} %get-tuple-element.43), kind=kCustom, calls=%fused_computation.2 | custom fusion | bytes 6316032 | tf_op jit(solution)/shard_map/gather | solution.py:223
  475.5 60.5 %reduce-scatter.21.cloned.1.call-done = f32[1536,128]{1,0:T(8,128)} async-done(((f32[6144,128]{1,0:T(8,128)}), f32[1536,128]{1,0:T(8,128)}) %reduce-scatter.21.cloned.1.call-update) | async-done | bytes 786448 | tf_op jit(solution)/shard_map/reduce_scatter | solution.py:60
  538.6 63.5 %all-gather.8.cloned.1.call-done = bf16[6144,256]{1,0:T(8,128)(2,1)} async-done(((bf16[1536,256]{1,0:T(8,128)(2,1)}), bf16[6144,256]{1,0:T(8,128)(2,1)}) %all-gather.8.cloned.1.call-update) | async-done | bytes 3145744 | tf_op jit(solution)/shard_map/all_gather | solution.py:56
  609.4 19.0 %gather_fusion.3 = f32[4096,256]{1,0:T(8,128)} fusion(f32[6144,256]{1,0:T(8,128)} %bitcast.137, s32[4096]{0:T(1024)S(1)} %broadcast_clamp_fusion), kind=kCustom, calls=%fused_computation.3 | custom fusion | bytes 8404992 | tf_op jit(solution)/shard_map/gather | solution.py:251
  632.6 20.3 %reduce-scatter.23.cloned.1.call-done = f32[128,256]{1,0:T(8,128)} async-done(((f32[512,256]{1,0:T(8,128)}), f32[128,256]{1,0:T(8,128)}) %reduce-scatter.23.cloned.1.call-update) | async-done | bytes 131088 | tf_op jit(solution)/shard_map/reduce_scatter | solution.py:69
  673.5 19.2 %reduce-scatter.25.cloned.1.call-done = f32[128,256]{1,0:T(8,128)} async-done(((f32[512,256]{1,0:T(8,128)}), f32[128,256]{1,0:T(8,128)}) %reduce-scatter.25.cloned.1.call-update) | async-done | bytes 131088 | tf_op jit(solution)/shard_map/reduce_scatter | solution.py:60
  703.2 14.4 %reduce-scatter.27.cloned.1.call-done = f32[128,256]{0,1:T(8,128)} async-done(((f32[512,256]{0,1:T(8,128)}), f32[128,256]{0,1:T(8,128)}) %reduce-scatter.27.cloned.1.call-update) | async-done | bytes 131088 | tf_op jit(solution)/shard_map/reduce_scatter | solution.py:60
  719.3 14.0 %all_gather.35 = bf16[512,512]{0,1:T(8,128)(2,1)S(1)} all-gather(bf16[128,512]{0,1:T(8,128)(2,1)S(1)} %bitcast.158), channel_id=1, replica_groups=mesh['dp'=2,'row'=4,'col'=4] {'row'}, dimensions={0}, use_global_device_ids=true | all-gather | bytes 655360 | tf_op jit(solution)/shard_map/all_gather | solution.py:56
  753.1 26.0 %all-reduce.5.cloned.1.call-done = (bf16[256,512]{1,0:T(8,128)(2,1)}, bf16[256,256]{1,0:T(8,128)(2,1)}) async-done(((bf16[256,512]{1,0:T(8,128)(2,1)}, bf16[256,256]{1,0:T(8,128)(2,1)}), (bf16[256,512]{1,0:T(8,128)(2,1)}, bf16[256,256]{1,0:T(8,128)(2,1)})) %all-reduce.5.cloned.1.call-update) | async-done | bytes 393232 | tf_op jit(solution)/shard_map/psum | solution.py:320
  782.8 31.0 %reduce-scatter.31.cloned.1.call-done = bf16[16,256,128]{2,1,0:T(8,128)(2,1)} async-done(((bf16[32,256,128]{2,1,0:T(8,128)(2,1)}), bf16[16,256,128]{2,1,0:T(8,128)(2,1)}) %reduce-scatter.31.cloned.1.call-update) | async-done | bytes 1048592 | tf_op jit(solution)/shard_map/reduce_scatter | solution.py:327
  816.5 31.8 %reduce-scatter.33.cloned.1.call-done = bf16[16,256,128]{2,1,0:T(8,128)(2,1)} async-done(((bf16[32,256,128]{2,1,0:T(8,128)(2,1)}), bf16[16,256,128]{2,1,0:T(8,128)(2,1)}) %reduce-scatter.33.cloned.1.call-update) | async-done | bytes 1048592 | tf_op jit(solution)/shard_map/reduce_scatter | solution.py:330
  851.1 21.3 %reduce-scatter.29.cloned.1.call-done = f32[128,256]{1,0:T(8,128)} async-done(((f32[512,256]{1,0:T(8,128)}), f32[128,256]{1,0:T(8,128)}) %reduce-scatter.29.cloned.1.call-update) | async-done | bytes 131088 | tf_op jit(solution)/shard_map/reduce_scatter | solution.py:69
  885.2 23.3 %all-reduce = (f32[256]{0:T(256)}, f32[256]{0:T(256)}, f32[256,32]{0,1:T(8,128)}) all-reduce(f32[256]{0:T(256)S(1)} %get-tuple-element.12, f32[256]{0:T(256)S(1)} %copy-done.52, f32[256,32]{0,1:T(8,128)S(1)} %fusion.44), channel_id=1, replica_groups=mesh['dp'=2,'row'=4,'col'=4] {'dp','col'}, use_global_device_ids=true, to_apply=%region_34.35 | all-reduce | flops 8704 | bytes 69632 | tf_op jit(solution)/shard_map/psum | solution.py:323
  (261 shorter events, 198.8 us)
Async XLA Ops:
  7.2 320.7 %copy-start = (bf16[32,128,256]{2,1,0:T(8,128)(2,1)S(1)}, bf16[32,128,256]{2,1,0:T(8,128)(2,1)}, u32[]{:S(2)}) copy-start(bf16[32,128,256]{2,1,0:T(8,128)(2,1)} %param.19) | copy-start | bytes 6291460
  7.2 50.5 %reduce-scatter.13.cloned.1.call-start = ((), (), s32[]{:S(2)}) async-start(), calls=%async_computation.12 | async-start | bytes 1310720 | tf_op jit(solution)/shard_map/reduce_scatter | solution.py:60
  32.1 96.2 %reduce-scatter.15.cloned.1.call-start = ((), (), s32[]{:S(2)}) async-start(), calls=%async_computation.13 | async-start | bytes 655360 | tf_op jit(solution)/shard_map/reduce_scatter | solution.py:69
  90.5 197.3 %reduce-scatter.17.cloned.1.call-start = ((), (), s32[]{:S(2)}) async-start(), calls=%async_computation.14 | async-start | bytes 7864320 | tf_op jit(solution)/shard_map/reduce_scatter | solution.py:185
  177.3 113.0 %copy-start.34 = (s32[4096,1]{0,1:T(1,128)S(1)}, s32[4096,1]{0,1:T(1,128)}, u32[]{:S(2)}) copy-start(s32[4096,1]{0,1:T(1,128)} %copy-done.33) | copy-start | bytes 49156
  177.3 150.6 %all-gather.4.cloned.1.call-start = ((), (), s32[]{:S(2)}) async-start(), calls=%async_computation.15 | async-start | bytes 1966080 | tf_op jit(solution)/shard_map/all_gather | solution.py:56
  290.2 105.3 %reduce-scatter.19.cloned.1.call-start = ((), (), s32[]{:S(2)}) async-start(), calls=%async_computation.16 | async-start | bytes 5242880 | tf_op jit(solution)/shard_map/reduce_scatter | solution.py:69
  351.9 92.4 %all-gather.6.cloned.1.call-start = ((), (), s32[]{:S(2)}) async-start(), calls=%async_computation.17 | async-start | bytes 2621440 | tf_op jit(solution)/shard_map/all_gather | solution.py:52
  424.3 111.8 %reduce-scatter.21.cloned.1.call-start = ((), (), s32[]{:S(2)}) async-start(), calls=%async_computation.18 | async-start | bytes 3932160 | tf_op jit(solution)/shard_map/reduce_scatter | solution.py:60
  475.5 126.6 %all-gather.8.cloned.1.call-start = ((), (), s32[]{:S(2)}) async-start(), calls=%async_computation.19 | async-start | bytes 3932160 | tf_op jit(solution)/shard_map/all_gather | solution.py:56
  538.5 114.4 %reduce-scatter.23.cloned.1.call-start = ((), (), s32[]{:S(2)}) async-start(), calls=%async_computation.20 | async-start | bytes 655360 | tf_op jit(solution)/shard_map/reduce_scatter | solution.py:69
  632.5 60.2 %reduce-scatter.25.cloned.1.call-start = ((), (), s32[]{:S(2)}) async-start(), calls=%async_computation.21 | async-start | bytes 655360 | tf_op jit(solution)/shard_map/reduce_scatter | solution.py:60
  673.4 44.1 %reduce-scatter.27.cloned.1.call-start = ((), (), s32[]{:S(2)}) async-start(), calls=%async_computation.22 | async-start | bytes 655360 | tf_op jit(solution)/shard_map/reduce_scatter | solution.py:60
  697.3 53.0 %reduce-scatter.35.cloned.1.call-start = ((), (), s32[]{:S(2)}) async-start(), calls=%async_computation.26 | async-start | bytes 3145728 | tf_op jit(solution)/shard_map/reduce_scatter | solution.py:333
  702.0 77.2 %all-reduce.5.cloned.1.call-start = ((), (), s32[]{:S(2)}) async-start(), calls=%async_computation.27 | async-start | bytes 786432 | tf_op jit(solution)/shard_map/psum | solution.py:320
  734.4 79.4 %reduce-scatter.31.cloned.1.call-start = ((), (), s32[]{:S(2)}) async-start(), calls=%async_computation.24 | async-start | bytes 3145728 | tf_op jit(solution)/shard_map/reduce_scatter | solution.py:327
  742.0 106.3 %reduce-scatter.33.cloned.1.call-start = ((), (), s32[]{:S(2)}) async-start(), calls=%async_computation.25 | async-start | bytes 3145728 | tf_op jit(solution)/shard_map/reduce_scatter | solution.py:330
  742.6 129.8 %reduce-scatter.29.cloned.1.call-start = ((), (), s32[]{:S(2)}) async-start(), calls=%async_computation.23 | async-start | bytes 655360 | tf_op jit(solution)/shard_map/reduce_scatter | solution.py:69
  781.0 129.2 %copy-start.1 = (bf16[32,128,256]{2,1,0:T(8,128)(2,1)S(1)}, bf16[32,128,256]{2,1,0:T(8,128)(2,1)}, u32[]{:S(2)}) copy-start(bf16[32,128,256]{2,1,0:T(8,128)(2,1)} %param.19) | copy-start | bytes 6291460
  782.7 89.7 %copy-start.51 = (f32[128]{0:T(128)S(1)}, f32[128]{0:T(128)}, u32[]{:S(2)}) copy-start(f32[128]{0:T(128)} %copy-done.50) | copy-start | bytes 1540
  782.7 102.5 %copy-start.52 = (f32[256]{0:T(256)S(1)}, f32[256]{0:T(256)}, u32[]{:S(2)}) copy-start(f32[256]{0:T(256)} %get-tuple-element.10) | copy-start | bytes 3076
  782.7 125.7 %copy-start.12 = (f32[128,256]{1,0:T(8,128)S(1)}, f32[128,256]{1,0:T(8,128)}, u32[]{:S(2)}) copy-start(f32[128,256]{1,0:T(8,128)} %copy-done.11) | copy-start | bytes 393220
  782.8 125.7 %copy-start.23 = (bf16[128,256]{1,0:T(8,128)(2,1)S(1)}, bf16[128,256]{1,0:T(8,128)(2,1)}, u32[]{:S(2)}) copy-start(bf16[128,256]{1,0:T(8,128)(2,1)} %param.21) | copy-start | bytes 196612
  782.8 125.7 %copy-start.55 = (f32[128]{0:T(128)S(1)}, f32[128]{0:T(128)}, u32[]{:S(2)}) copy-start(f32[128]{0:T(128)} %copy-done.54) | copy-start | bytes 1540
  (48 other events, 957.2 us)
Sparse Core Ops, SparseCore 0:
  32.2 25.4 reduce-scatter.12
  90.7 20.1 reduce-scatter.14
  177.4 110.3 reduce-scatter.16
  290.3 37.5 all-gather.3
  352.0 43.4 reduce-scatter.18
  424.4 19.8 all-gather.5
  475.6 60.3 reduce-scatter.20
  538.7 63.3 all-gather.7
  632.6 20.2 reduce-scatter.22
  673.5 19.0 reduce-scatter.24
  697.4 20.1 reduce-scatter.26
  720.2 30.0 reduce-scatter.34
  753.3 25.7 all-reduce.4
  781.8 31.8 reduce-scatter.30
  816.4 31.8 reduce-scatter.32
  850.7 21.6 reduce-scatter.28
where the time goes:
time: 919 us; the launch traced here: 917 us
  waiting for transfers between devices  515 us (56%)
  local copies, waits for them, and re-layouts  145 us (16%)
  blocking collectives  145 us (16%)
  other arithmetic  48.8 us (5%)
  matrix products  46.4 us (5%)
  between operations  14.8 us (2%)
    reduce_scatter x1, waiting for transfers between devices, per_device(): lax.psum_scatter(jnp.einsum('ecd,edf->ecf', row_block, w_both, preferred_...  110 us
    reduce_scatter x4, waiting for transfers between devices, row_terms(): lax.psum_scatter(term_maker(jnp.int32(0), local_rows * lax.axis_size('row...  107 us
    all_gather x2, waiting for transfers between devices, row_rows(): return lax.all_gather(block_array, 'row', axis=0, tiled=True)  101 us
    reduce_scatter x4, waiting for transfers between devices, col_terms(): lax.psum_scatter(term_maker(jnp.int32(0), local_rows * lax.axis_size('col...  82.2 us
    all_gather x3, blocking collectives, row_rows(): return lax.all_gather(block_array, 'row', axis=0, tiled=True)  39.8 us
    psum x3, blocking collectives, row_total(): return lax.psum(partial_sum, 'row')  36.8 us
    reduce_scatter x1, waiting for transfers between devices, per_device(): lax.psum_scatter(both_grad[:, :, ffn_local:].astype(jnp.bfloat16), 'dp',...  31.8 us
    reduce_scatter x1, waiting for transfers between devices, per_device(): lax.psum_scatter(both_grad[:, :, :ffn_local].astype(jnp.bfloat16), 'dp',...  31 us
  transfers between devices with their start and end apart: 16, of which 15 were waited for; matrix products, arithmetic and copies ran while one was open for 9% of the time, Pallas kernels for 0%

commit v1 on v0

--- a/solution.py
+++ b/solution.py
@@ -7,6 +7,7 @@
 KV_HEADS = 8
 HEAD_DIM = 64
 CAP = 192
+EXPERTS = 32
 
 
 epsilon = 1e-06
@@ -348,6 +349,278 @@
     )
 
 
+def from_blocks(blocks):
+    row_blocks, col_blocks, height, width = blocks.shape
+    return blocks.transpose(0, 2, 1, 3).reshape(row_blocks * height, col_blocks * width)
+
+
+def to_blocks(full_array, height, width):
+    rows, cols = full_array.shape
+    return full_array.reshape(rows // height, height, cols // width, width).transpose(0, 2, 1, 3)
+
+
+def expert_owner(
+    block_input, attn_gain, w_qkv, w_out, ffn_gain, w_router, w_gate, w_up, w_down, routes, out_grad
+):
+    tok_local, width_local = block_input.shape
+    dp_size, row_size, col_size = (lax.axis_size(name) for name in ("dp", "row", "col"))
+    model_width = width_local * row_size
+    seq_len = routes.shape[0]
+    tokens = seq_len * dp_size
+    experts = w_gate.shape[0]
+    ffn_local = w_gate.shape[2]
+    ffn = ffn_local * col_size
+    repeat = HEADS // KV_HEADS
+    groups_local = KV_HEADS // col_size
+    head_cols = groups_local * repeat * HEAD_DIM
+    dp_index, row_index, col_index = (lax.axis_index(name) for name in ("dp", "row", "col"))
+    score_scale = HEAD_DIM ** (-0.5)
+    everyone = ("dp", "col", "row")
+    peers = ("row", "col")
+    owned = experts // dp_size
+    own_expert = dp_index * owned + row_index * col_size + col_index
+    token_blocks = dp_size * col_size
+    tok_share = tokens // (token_blocks * row_size)
+    seq_first = dp_index * seq_len
+    block_first = (dp_index * col_size + col_index) * tok_local
+    share_first = block_first + row_index * tok_share
+    width_first = row_index * width_local
+
+    def rows_of(full_array, first_row, count):
+        return lax.dynamic_slice_in_dim(full_array, first_row, count, 0)
+
+    def cols_of(full_array, first_col, count):
+        return lax.dynamic_slice_in_dim(full_array, first_col, count, 1)
+
+    def whole(block_array):
+        gathered = lax.all_gather(block_array, everyone, axis=0)
+        return from_blocks(gathered.reshape(token_blocks, row_size, tok_local, width_local))
+
+    inputs_f = whole(block_input).astype(jnp.float32)
+    w_qkv_all = lax.all_gather(w_qkv, "row", axis=0, tiled=True)
+    small = jnp.concatenate([w_router, attn_gain[:, None], ffn_gain[:, None]], axis=1)
+    small_all = lax.all_gather(small, "row", axis=0, tiled=True)
+    w_router_all = small_all[:, :experts]
+    attn_gain_all = small_all[:, experts]
+    ffn_gain_all = small_all[:, experts + 1]
+    routes_all = lax.all_gather(routes, "dp", axis=0, tiled=True)
+    w_out_all = from_blocks(
+        lax.all_gather(w_out, ("col", "row"), axis=0).reshape(
+            col_size, row_size, w_out.shape[0], width_local
+        )
+    )
+    grad_f = whole(out_grad).astype(jnp.float32)
+
+    def own_weight(weight):
+        mine = lax.dynamic_slice_in_dim(weight, dp_index * owned, owned, 0)
+        moved = lax.all_to_all(mine, peers, 0, 0, tiled=True)
+        return moved.reshape((row_size, col_size) + weight.shape[1:])
+
+    gate_own = from_blocks(own_weight(w_gate))
+    up_own = from_blocks(own_weight(w_up))
+    down_own = from_blocks(own_weight(w_down).transpose(1, 0, 2, 3))
+
+    inv_rms_one = lax.rsqrt(jnp.mean(inputs_f * inputs_f, axis=1, keepdims=True) + epsilon)
+    unit_one = inputs_f * inv_rms_one
+    normed_one = (unit_one * attn_gain_all).astype(jnp.bfloat16)
+    normed_seq = rows_of(normed_one, seq_first, seq_len)
+    proj_flat = jnp.dot(normed_seq, w_qkv_all, preferred_element_type=jnp.float32)
+    proj_qkv = proj_flat.reshape(seq_len, groups_local, repeat + 2, HEAD_DIM)
+    positions = jnp.arange(seq_len, dtype=jnp.int32)
+    cos_table, sin_table = rope_tables(positions, HEAD_DIM)
+    queries = proj_qkv[:, :, :repeat]
+    keys_raw = proj_qkv[:, :, repeat]
+    values_all = proj_qkv[:, :, repeat + 1].astype(jnp.bfloat16)
+    queries_rot = (
+        (queries * cos_table[:, None, None] + rotate_half(queries) * sin_table[:, None, None])
+        * score_scale
+    ).astype(jnp.bfloat16)
+    keys_all = (keys_raw * cos_table[:, None] + rotate_half(keys_raw) * sin_table[:, None]).astype(
+        jnp.bfloat16
+    )
+    causal = positions[None, :] <= positions[:, None]
+    scores = jnp.einsum("qgrd,kgd->grqk", queries_rot, keys_all, preferred_element_type=jnp.float32)
+    exp_scores = jnp.where(causal, jnp.exp(scores), 0.0)
+    log_total = jnp.log(jnp.sum(exp_scores, axis=-1, keepdims=True))
+    attn_probs = jnp.where(causal, jnp.exp(scores - log_total), 0.0)
+    probs_b = attn_probs.astype(jnp.bfloat16)
+    attended = (
+        jnp.einsum("grqk,kgd->qgrd", probs_b, values_all, preferred_element_type=jnp.float32)
+        .astype(jnp.bfloat16)
+        .reshape(seq_len, head_cols)
+    )
+    attended_all = from_blocks(
+        lax.all_gather(attended, ("dp", "col"), axis=0).reshape(
+            dp_size, col_size, seq_len, head_cols
+        )
+    )
+    hidden_res = inputs_f + jnp.dot(attended_all, w_out_all, preferred_element_type=jnp.float32)
+    inv_rms_two = lax.rsqrt(jnp.mean(hidden_res * hidden_res, axis=1, keepdims=True) + epsilon)
+    unit_two = hidden_res * inv_rms_two
+    normed_two_f = unit_two * ffn_gain_all
+    normed_two = normed_two_f.astype(jnp.bfloat16)
+    logits = jnp.dot(normed_two_f, w_router_all, precision=lax.Precision.HIGHEST)
+    chosen_mask = jnp.any(
+        routes_all[:, :, None] == jnp.arange(experts, dtype=jnp.int32)[None, None, :], axis=1
+    )
+    exp_chosen = jnp.where(chosen_mask, jnp.exp(logits), 0.0)
+    gate_weights = exp_chosen / jnp.sum(exp_chosen, axis=1, keepdims=True)
+    gate_own_weight = cols_of(gate_weights, own_expert, 1)
+
+    gate_pre = jnp.dot(normed_two, gate_own, preferred_element_type=jnp.float32)
+    up_val = jnp.dot(normed_two, up_own, preferred_element_type=jnp.float32)
+    sigmoid_gate = jax.nn.sigmoid(gate_pre)
+    activated = (gate_pre * sigmoid_gate * up_val).astype(jnp.bfloat16)
+    pair_out = jnp.dot(activated, down_own, preferred_element_type=jnp.float32)
+    gate_grads = lax.all_gather(
+        jnp.sum(grad_f * pair_out, axis=1), ("dp", "row", "col"), axis=0
+    ).T
+    gate_mix = gate_weights * (
+        gate_grads - jnp.sum(gate_weights * gate_grads, axis=1, keepdims=True)
+    )
+    pair_grad = (gate_own_weight * grad_f).astype(jnp.bfloat16)
+    act_grad = lax.dot_general(
+        pair_grad, down_own, (((1,), (1,)), ((), ())), preferred_element_type=jnp.float32
+    )
+    gate_pre_grad = (
+        act_grad * up_val * sigmoid_gate * (1.0 + gate_pre * (1.0 - sigmoid_gate))
+    ).astype(jnp.bfloat16)
+    up_grad = (act_grad * gate_pre * sigmoid_gate).astype(jnp.bfloat16)
+    token_back = lax.dot_general(
+        gate_pre_grad, gate_own, (((1,), (1,)), ((), ())), preferred_element_type=jnp.float32
+    ) + lax.dot_general(
+        up_grad, up_own, (((1,), (1,)), ((), ())), preferred_element_type=jnp.float32
+    )
+    back_share = lax.psum_scatter(
+        token_back.astype(jnp.bfloat16), everyone, scatter_dimension=0, tiled=True
+    ).astype(jnp.float32)
+    moe_block = lax.psum_scatter(
+        to_blocks(
+            (gate_own_weight * pair_out).astype(jnp.bfloat16), tok_local, width_local
+        ).reshape(token_blocks * row_size, tok_local, width_local),
+        everyone,
+        scatter_dimension=0,
+        tiled=True,
+    ).reshape(tok_local, width_local)
+    own_hidden = cols_of(rows_of(hidden_res, block_first, tok_local), width_first, width_local)
+    block_output = (own_hidden + moe_block.astype(jnp.float32)).astype(jnp.bfloat16)
+
+    normed_grad = back_share + jnp.dot(
+        rows_of(gate_mix, share_first, tok_share), w_router_all.T, precision=lax.Precision.HIGHEST
+    )
+    unit_share = rows_of(unit_two, share_first, tok_share)
+    ffn_gain_part = jnp.sum(normed_grad * unit_share, axis=0)
+    unit_grad_two = normed_grad * ffn_gain_all
+    residual_share = rows_of(grad_f, share_first, tok_share) + rows_of(
+        inv_rms_two, share_first, tok_share
+    ) * (unit_grad_two - unit_share * jnp.mean(unit_grad_two * unit_share, axis=1, keepdims=True))
+    residual_all = lax.all_gather(
+        residual_share.astype(jnp.bfloat16), everyone, axis=0, tiled=True
+    )
+
+    def expert_grad(blocks):
+        return lax.all_to_all(blocks, peers, 0, 0, tiled=True).astype(jnp.float32)
+
+    def turned(left, right):
+        return lax.dot_general(
+            left, right, (((0,), (0,)), ((), ())), preferred_element_type=jnp.float32
+        )
+
+    def sent(blocks):
+        return blocks.reshape((row_size * col_size,) + blocks.shape[2:])
+
+    grad_down = expert_grad(
+        sent(
+            to_blocks(
+                turned(activated, pair_grad).astype(jnp.bfloat16), ffn_local, width_local
+            ).transpose(1, 0, 2, 3)
+        )
+    )
+    grad_gate = expert_grad(
+        sent(to_blocks(turned(normed_two, gate_pre_grad).astype(jnp.bfloat16), width_local, ffn_local))
+    )
+    grad_up = expert_grad(
+        sent(to_blocks(turned(normed_two, up_grad).astype(jnp.bfloat16), width_local, ffn_local))
+    )
+    grad_router = lax.dot_general(
+        cols_of(normed_two_f, width_first, width_local),
+        gate_mix,
+        (((0,), (0,)), ((), ())),
+        precision=lax.Precision.HIGHEST,
+    )
+
+    grad_out = turned(
+        cols_of(attended_all, col_index * head_cols, head_cols),
+        cols_of(residual_all, width_first, width_local),
+    )
+    attended_grad = (
+        lax.dot_general(
+            rows_of(residual_all, seq_first, seq_len),
+            rows_of(w_out_all, col_index * head_cols, head_cols),
+            (((1,), (1,)), ((), ())),
+            preferred_element_type=jnp.float32,
+        )
+        .astype(jnp.bfloat16)
+        .reshape(seq_len, groups_local, repeat, HEAD_DIM)
+    )
+    prob_grad = jnp.einsum(
+        "qgrd,kgd->grqk", attended_grad, values_all, preferred_element_type=jnp.float32
+    )
+    prob_inner = jnp.sum(attn_probs * prob_grad, axis=-1, keepdims=True)
+    score_grad = (attn_probs * (prob_grad - prob_inner)).astype(jnp.bfloat16)
+    query_grad = jnp.einsum(
+        "grqk,kgd->qgrd", score_grad, keys_all, preferred_element_type=jnp.float32
+    )
+    key_grad = jnp.einsum(
+        "grqk,qgrd->kgd", score_grad, queries_rot, preferred_element_type=jnp.float32
+    )
+    value_grad = jnp.einsum(
+        "grqk,qgrd->kgd", probs_b, attended_grad, preferred_element_type=jnp.float32
+    )
+    query_back = (
+        query_grad * cos_table[:, None, None] - rotate_half(query_grad * sin_table[:, None, None])
+    ) * score_scale
+    key_back = key_grad * cos_table[:, None] - rotate_half(key_grad * sin_table[:, None])
+    qkv_grad = (
+        jnp.concatenate([query_back, key_back[:, :, None], value_grad[:, :, None]], axis=2)
+        .reshape(seq_len, -1)
+        .astype(jnp.bfloat16)
+    )
+    grad_qkv = lax.psum(
+        turned(cols_of(normed_seq, width_first, width_local), qkv_grad).astype(jnp.bfloat16), "dp"
+    ).astype(jnp.float32)
+    norm_back = lax.dot_general(
+        qkv_grad, w_qkv, (((1,), (1,)), ((), ())), preferred_element_type=jnp.float32
+    )
+    unit_own = cols_of(rows_of(unit_one, seq_first, seq_len), width_first, width_local)
+    attn_gain_part = jnp.sum(norm_back * unit_own, axis=0)
+    inner_part = jnp.sum(qkv_grad.astype(jnp.float32) * proj_flat, axis=1, keepdims=True)
+    input_part = rows_of(inv_rms_one, seq_first, seq_len) * (
+        norm_back * attn_gain - unit_own * (inner_part / model_width)
+    )
+    own_residual = cols_of(rows_of(residual_all, block_first, tok_local), width_first, width_local)
+    input_grad = own_residual.astype(jnp.float32) + lax.psum_scatter(
+        input_part, "col", scatter_dimension=0, tiled=True
+    )
+    attn_gain_wide = lax.dynamic_update_slice_in_dim(
+        jnp.zeros((model_width,), jnp.float32), attn_gain_part, width_first, 0
+    )
+    gains = lax.psum(jnp.stack([attn_gain_wide, ffn_gain_part]), ("dp", "row", "col"))
+    gains_own = cols_of(gains, width_first, width_local)
+    return (
+        block_output,
+        input_grad,
+        gains_own[0],
+        grad_qkv,
+        grad_out,
+        gains_own[1],
+        grad_router,
+        grad_gate,
+        grad_up,
+        grad_down,
+    )
+
+
 def solution(mesh):
     in_specs = (
         P(("dp", "col"), "row"),
@@ -374,6 +647,8 @@
         P("dp", "row", "col"),
         P("dp", "col", "row"),
     )
+    sizes = dict(mesh.shape)
+    one_expert_each = sizes["dp"] * sizes["row"] * sizes["col"] == EXPERTS
     return jax.shard_map(
-        per_device, mesh=mesh, in_specs=in_specs, out_specs=out_specs, check_vma=False
-    )
+        expert_owner if one_expert_each else per_device, mesh=mesh, in_specs=in_specs, out_specs=out_specs, check_vma=False
+    )

time: 919 us -> 748 us (0.81)
  waiting for transfers between devices: 515 us -> 393 us
  local copies, waits for them, and re-layouts: 145 us -> 65.3 us
  starting transfers between devices: 0.84 us -> 37.1 us
  blocking collectives: 145 us -> 121 us
  matrix products: 46.4 us -> 65.7 us
    reduce_scatter x12 -> x3, waiting for transfers between devices: 368 us -> 207 us  [the longest x1 135 us: expert_owner(): lax.psum_scatter(token_back.astype(jnp.bfloat16), everyone, scatter_dimen...]
    gather x4 -> x0, local copies, waits for them, and re-layouts: 92.2 us -> none  [the longest x1 27.4 us: per_device(): slot_grad = jnp.where(filled[:, None] > 0, pair_grad_all[pair_of_slot], 0)]
    all_to_all x0 -> x6, waiting for transfers between devices: none -> 65.4 us  [the longest x3 36.6 us: own_weight(): moved = lax.all_to_all(mine, peers, 0, 0, tiled=True)]
    psum x6 -> x1, blocking collectives: 88.1 us -> 37.9 us  [expert_owner(): lax.psum(jnp.stack([attn_gain_wide, ffn_gain_part]), ('dp', 'row', 'col'))]
    all_to_all x0 -> x6, starting transfers between devices: none -> 36.3 us  [the longest x3 18.3 us: own_weight(): moved = lax.all_to_all(mine, peers, 0, 0, tiled=True)]
    scatter x2 -> x0, local copies, waits for them, and re-layouts: 31.1 us -> none  [the longest x1 15.5 us: slot_tables(): pair_of_slot = jnp.zeros((experts * capacity,), jnp.int32).at[slot_of_pai...]
    all_gather x6 -> x3, blocking collectives: 57.1 us -> 83.3 us  [the longest x1 44 us: expert_owner(): lax.all_gather(jnp.sum(grad_f * pair_out, axis=1), ('dp', 'row', 'col'),...]
    psum x1, waiting for transfers between devices: 26 us -> 0.01 us  [expert_owner(): lax.psum(turned(cols_of(normed_seq, width_first, width_local), qkv_grad)....]
  transfers between devices with their start and end apart: 16 -> 16, of which waited for: 15 -> 12; matrix products, arithmetic and copies ran while one was open for 9% -> 17% of each run, Pallas kernels for 0% -> 0%
where the time goes in v1:
time: 748 us; the launch traced here: 739 us
  waiting for transfers between devices  393 us (53%)
  blocking collectives  121 us (16%)
  matrix products  65.7 us (9%)
  local copies, waits for them, and re-layouts  65.3 us (9%)
  other arithmetic  41.5 us (6%)
  starting transfers between devices  37.1 us (5%)
  between operations  15.2 us (2%)
    reduce_scatter x1, waiting for transfers between devices, expert_owner(): lax.psum_scatter(token_back.astype(jnp.bfloat16), everyone, scatter_dimen...  135 us
    reduce_scatter x1, waiting for transfers between devices, expert_owner(): lax.psum_scatter(to_blocks((gate_own_weight * pair_out).astype(jnp.bfloat...  66.9 us
    all_gather x2, waiting for transfers between devices, whole(): gathered = lax.all_gather(block_array, everyone, axis=0)  61.8 us
    all_gather x1, blocking collectives, expert_owner(): lax.all_gather(jnp.sum(grad_f * pair_out, axis=1), ('dp', 'row', 'col'),...  44 us
    psum x1, blocking collectives, expert_owner(): lax.psum(jnp.stack([attn_gain_wide, ffn_gain_part]), ('dp', 'row', 'col'))  37.9 us
    all_to_all x3, waiting for transfers between devices, own_weight(): moved = lax.all_to_all(mine, peers, 0, 0, tiled=True)  36.6 us
    all_gather x1, blocking collectives, expert_owner(): small_all = lax.all_gather(small, 'row', axis=0, tiled=True)  34.7 us
    all_to_all x3, waiting for transfers between devices, expert_grad(): return lax.all_to_all(blocks, peers, 0, 0, tiled=True).astype(jnp.float32)  28.8 us
  transfers between devices with their start and end apart: 16, of which 12 were waited for; matrix products, arithmetic and copies ran while one was open for 17% of the time, Pallas kernels for 0%

profile of v1, /device:TPU:0, one launch (start us, length us, event | category | flops | bytes accessed | tf_op | source)
XLA Modules:
  0.0 739.1 jit_solution(880390796690062235)
XLA Ops:
  11.1 7.4 %all-to-all-start = ((bf16[16,256,128]{2,1,0:T(8,128)(2,1)}), bf16[16,256,128]{2,1,0:T(8,128)(2,1)}, u32[]{:S(2)}, u32[]{:S(2)}) async-start(bf16[16,256,128]{2,1,0:T(8,128)(2,1)} %constant_dynamic-slice_fusion.4), calls=%async_computation | async-start | bytes 2097152 | tf_op jit(solution)/shard_map/all_to_all | solution.py:416
  18.6 34.7 %all_gather.41 = f32[1024,34]{0,1:T(8,128)S(1)} all-gather(f32[256,34]{0,1:T(8,128)S(1)} %pad_maximum_fusion.3), channel_id=1, replica_groups=mesh['dp'=2,'row'=4,'col'=4] {'row'}, dimensions={0}, use_global_device_ids=true | all-gather | bytes 174080 | tf_op jit(solution)/shard_map/all_gather | solution.py:402
  56.8 19.8 %all-gather.17.cloned.1.call-done = bf16[4096,256]{1,0:T(8,128)(2,1)} async-done(((bf16[128,256]{1,0:T(8,128)(2,1)}), bf16[4096,256]{1,0:T(8,128)(2,1)}) %all-gather.17.cloned.1.call-update) | async-done | bytes 2097168 | tf_op jit(solution)/shard_map/all_gather | solution.py:396
  84.2 4.7 multiply_convert_fusion.3
  89.0 16.0 %all-gather.11.cloned.1.call-done = bf16[1024,512]{1,0:T(8,128)(2,1)} async-done(((bf16[256,512]{1,0:T(8,128)(2,1)}), bf16[1024,512]{1,0:T(8,128)(2,1)}) %all-gather.11.cloned.1.call-update) | async-done | bytes 1048592 | tf_op jit(solution)/shard_map/all_gather | solution.py:400
  118.7 20.5 %all-to-all-done.1 = bf16[16,256,128]{2,1,0:T(8,128)(2,1)S(1)} async-done(((bf16[16,256,128]{2,1,0:T(8,128)(2,1)}), bf16[16,256,128]{2,1,0:T(8,128)(2,1)S(1)}, u32[]{:S(2)}, u32[]{:S(2)}) %all-to-all-start.1) | async-done | bytes 1048608 | tf_op jit(solution)/shard_map/all_to_all | solution.py:416
  139.1 6.8 all-to-all-start.2
  156.2 16.1 %all-to-all-done.2 = bf16[16,128,256]{2,1,0:T(8,128)(2,1)S(1)} async-done(((bf16[16,128,256]{2,1,0:T(8,128)(2,1)}), bf16[16,128,256]{2,1,0:T(8,128)(2,1)S(1)}, u32[]{:S(2)}, u32[]{:S(2)}) %all-to-all-start.2) | async-done | bytes 1048608 | tf_op jit(solution)/shard_map/all_to_all | solution.py:416
  179.3 42.0 %all-gather.21.cloned.1.call-done = bf16[4096,256]{1,0:T(8,128)(2,1)} async-done(((bf16[128,256]{1,0:T(8,128)(2,1)}), bf16[4096,256]{1,0:T(8,128)(2,1)}) %all-gather.21.cloned.1.call-update) | async-done | bytes 2097168 | tf_op jit(solution)/shard_map/all_gather | solution.py:396
  221.4 5.4 copy.134
  229.9 5.2 copy.161
  235.1 15.2 %all-gather.13.cloned.1.call-done = bf16[8,512,256]{2,1,0:T(8,128)(2,1)} async-done(((bf16[1,512,256]{2,1,0:T(8,128)(2,1)}), bf16[8,512,256]{2,1,0:T(8,128)(2,1)}) %all-gather.13.cloned.1.call-update) | async-done | bytes 2097168 | tf_op jit(solution)/shard_map/all_gather | solution.py:453
  271.7 44.0 %all-gather.3 = f32[32768]{0:T(1024)} all-gather(f32[1024]{0:T(1024)S(1)} %get-tuple-element.43), channel_id=5, replica_groups=mesh['dp'=2,'row'=4,'col'=4] {'dp','row','col'}, dimensions={0}, use_global_device_ids=true | all-gather | bytes 135168 | tf_op jit(solution)/shard_map/all_gather | solution.py:475
  316.6 6.3 fusion.98
  334.1 134.9 %reduce-scatter.6.cloned.1.call-done = bf16[32,1024]{1,0:T(8,128)(2,1)} async-done(((bf16[1024,1024]{1,0:T(8,128)(2,1)}), bf16[32,1024]{1,0:T(8,128)(2,1)}) %reduce-scatter.6.cloned.1.call-update) | async-done | bytes 65552 | tf_op jit(solution)/shard_map/reduce_scatter | solution.py:494
  506.9 25.2 %all-gather.15.cloned.1.call-done = bf16[1024,1024]{1,0:T(8,128)(2,1)} async-done(((bf16[32,1024]{1,0:T(8,128)(2,1)}), bf16[1024,1024]{1,0:T(8,128)(2,1)}) %all-gather.15.cloned.1.call-update) | async-done | bytes 2097168 | tf_op jit(solution)/shard_map/all_gather | solution.py:517
  542.0 6.0 fusion.3
  548.0 4.7 fusion.5
  555.6 16.8 %all-to-all-done.4 = bf16[16,256,128]{2,1,0:T(8,128)(2,1)} async-done(((bf16[16,256,128]{2,1,0:T(8,128)(2,1)}), bf16[16,256,128]{2,1,0:T(8,128)(2,1)}, u32[]{:S(2)}, u32[]{:S(2)}) %all-to-all-start.4) | async-done | bytes 1048608 | tf_op jit(solution)/shard_map/all_to_all | solution.py:522
  572.4 9.0 %all-to-all-start.5 = ((bf16[16,128,256]{2,1,0:T(8,128)(2,1)}), bf16[16,128,256]{2,1,0:T(8,128)(2,1)}, u32[]{:S(2)}, u32[]{:S(2)}) async-start(bf16[16,128,256]{2,1,0:T(8,128)(2,1)} %bitcast.232), calls=%async_computation.8 | async-start | bytes 2097152 | tf_op jit(solution)/shard_map/all_to_all | solution.py:522
  599.2 12.0 %all-to-all-done.5 = bf16[16,128,256]{2,1,0:T(8,128)(2,1)} async-done(((bf16[16,128,256]{2,1,0:T(8,128)(2,1)}), bf16[16,128,256]{2,1,0:T(8,128)(2,1)}, u32[]{:S(2)}, u32[]{:S(2)}) %all-to-all-start.5) | async-done | bytes 1048608 | tf_op jit(solution)/shard_map/all_to_all | solution.py:522
  614.1 66.9 %reduce-scatter.4.cloned.1.call-done = bf16[1,128,256]{2,1,0:T(8,128)(2,1)} async-done(((bf16[32,128,256]{2,1,0:T(8,128)(2,1)}), bf16[1,128,256]{2,1,0:T(8,128)(2,1)}) %reduce-scatter.4.cloned.1.call-update) | async-done | bytes 65552 | tf_op jit(solution)/shard_map/reduce_scatter | solution.py:497
  682.7 37.9 %psum.14 = f32[2,1024]{1,0:T(2,128)S(1)} all-reduce(f32[2,1024]{1,0:T(2,128)S(1)} %pad_maximum_fusion.4), channel_id=1, replica_groups=mesh['dp'=2,'row'=4,'col'=4] {'dp','row','col'}, use_global_device_ids=true, to_apply=%region_16.17 | all-reduce | flops 2048 | bytes 16384 | tf_op jit(solution)/shard_map/psum | solution.py:608
  725.3 5.0 reduce-scatter.8.cloned.1.call-done
  (214 shorter events, 161.3 us)
Async XLA Ops:
  7.2 69.4 %all-gather.17.cloned.1.call-start = ((), (), s32[]{:S(2)}) async-start(), calls=%async_computation.16 | async-start | bytes 2162688 | tf_op jit(solution)/shard_map/all_gather | solution.py:396
  7.9 97.1 %all-gather.11.cloned.1.call-start = ((), (), s32[]{:S(2)}) async-start(), calls=%async_computation.9 | async-start | bytes 1310720 | tf_op jit(solution)/shard_map/all_gather | solution.py:400
  8.7 165.6 %all-gather.19.cloned.1.call-start = ((), (), s32[]{:S(2)}) async-start(), calls=%async_computation.17 | async-start | bytes 2228224 | tf_op jit(solution)/shard_map/all_gather | solution.py:408
  9.4 211.9 %all-gather.21.cloned.1.call-start = ((), (), s32[]{:S(2)}) async-start(), calls=%async_computation.18 | async-start | bytes 2162688 | tf_op jit(solution)/shard_map/all_gather | solution.py:396
  10.0 8.6 %copy-start.38 = (f32[256,32]{0,1:T(8,128)S(1)}, f32[256,32]{0,1:T(8,128)}, u32[]{:S(2)}) copy-start(f32[256,32]{0,1:T(8,128)} %param.16) | copy-start | bytes 98308
  10.0 8.6 %copy-start.41 = (f32[256]{0:T(256)S(1)}, f32[256]{0:T(256)}, u32[]{:S(2)}) copy-start(f32[256]{0:T(256)} %param.12) | copy-start | bytes 3076
  11.1 96.8 %all-to-all-start = ((bf16[16,256,128]{2,1,0:T(8,128)(2,1)}), bf16[16,256,128]{2,1,0:T(8,128)(2,1)}, u32[]{:S(2)}, u32[]{:S(2)}) async-start(bf16[16,256,128]{2,1,0:T(8,128)(2,1)} %constant_dynamic-slice_fusion.4), calls=%async_computation | async-start | bytes 2097152 | tf_op jit(solution)/shard_map/all_to_all | solution.py:416
  89.0 18.7 %copy-start.11 = (bf16[1024,1024]{1,0:T(8,128)(2,1)}, bf16[1024,1024]{1,0:T(8,128)(2,1)S(1)}, u32[]{:S(2)}) copy-start(bf16[1024,1024]{1,0:T(8,128)(2,1)S(1)} %get-tuple-element.17) | copy-start | bytes 6291460
  108.0 31.2 %all-to-all-start.1 = ((bf16[16,256,128]{2,1,0:T(8,128)(2,1)}), bf16[16,256,128]{2,1,0:T(8,128)(2,1)S(1)}, u32[]{:S(2)}, u32[]{:S(2)}) async-start(bf16[16,256,128]{2,1,0:T(8,128)(2,1)} %constant_dynamic-slice_fusion.3), calls=%async_computation.1 | async-start | bytes 2097152 | tf_op jit(solution)/shard_map/all_to_all | solution.py:416
  112.1 138.3 %all-gather.13.cloned.1.call-start = ((), (), s32[]{:S(2)}) async-start(), calls=%async_computation.10 | async-start | bytes 2359296 | tf_op jit(solution)/shard_map/all_gather | solution.py:453
  116.4 29.6 %copy-start.39 = (s32[512,8]{0,1:T(8,128)S(1)}, s32[512,8]{0,1:T(8,128)}, u32[]{:S(2)}) copy-start(s32[512,8]{0,1:T(8,128)} %param.20) | copy-start | bytes 49156
  139.1 33.2 %all-to-all-start.2 = ((bf16[16,128,256]{2,1,0:T(8,128)(2,1)}), bf16[16,128,256]{2,1,0:T(8,128)(2,1)S(1)}, u32[]{:S(2)}, u32[]{:S(2)}) async-start(bf16[16,128,256]{2,1,0:T(8,128)(2,1)} %constant_dynamic-slice_fusion.2), calls=%async_computation.2 | async-start | bytes 2097152 | tf_op jit(solution)/shard_map/all_to_all | solution.py:416
  145.9 323.1 %reduce-scatter.6.cloned.1.call-start = ((), (), s32[]{:S(2)}) async-start(), calls=%async_computation.12 | async-start | bytes 2162688 | tf_op jit(solution)/shard_map/reduce_scatter | solution.py:494
  331.8 140.4 %copy-start.13 = (bf16[1024,1024]{1,0:T(8,128)(2,1)S(1)}, bf16[1024,1024]{1,0:T(8,128)(2,1)}, u32[]{:S(2)}) copy-start(bf16[1024,1024]{1,0:T(8,128)(2,1)} %copy-done.12) | copy-start | bytes 6291460
  331.8 200.3 %all-gather.15.cloned.1.call-start = ((), (), s32[]{:S(2)}) async-start(), calls=%async_computation.13 | async-start | bytes 2162688 | tf_op jit(solution)/shard_map/all_gather | solution.py:517
  478.2 59.1 %all-to-all-start.3 = ((bf16[16,256,128]{2,1,0:T(8,128)(2,1)}), bf16[16,256,128]{2,1,0:T(8,128)(2,1)}, u32[]{:S(2)}, u32[]{:S(2)}) async-start(bf16[16,256,128]{2,1,0:T(8,128)(2,1)} %bitcast.60), calls=%async_computation.6 | async-start | bytes 2097152 | tf_op jit(solution)/shard_map/all_to_all | solution.py:522
  482.6 198.4 %reduce-scatter.4.cloned.1.call-start = ((), (), s32[]{:S(2)}) async-start(), calls=%async_computation.11 | async-start | bytes 2162688 | tf_op jit(solution)/shard_map/reduce_scatter | solution.py:497
  537.3 35.1 %all-to-all-start.4 = ((bf16[16,256,128]{2,1,0:T(8,128)(2,1)}), bf16[16,256,128]{2,1,0:T(8,128)(2,1)}, u32[]{:S(2)}, u32[]{:S(2)}) async-start(bf16[16,256,128]{2,1,0:T(8,128)(2,1)} %bitcast.62), calls=%async_computation.7 | async-start | bytes 2097152 | tf_op jit(solution)/shard_map/all_to_all | solution.py:522
  555.6 25.9 %copy-start.26 = (bf16[512,2,2,64]{0,3,2,1:T(8,128)(2,1)S(1)}, bf16[512,2,2,64]{0,3,2,1:T(8,128)(2,1)}, u32[]{:S(2)}) copy-start(bf16[512,2,2,64]{0,3,2,1:T(8,128)(2,1)} %copy-done.23) | copy-start | bytes 786436
  555.6 25.9 %copy-start.36 = (bf16[512,256]{0,1:T(8,128)(2,1)S(1)}, bf16[512,256]{0,1:T(8,128)(2,1)}, u32[]{:S(2)}) copy-start(bf16[512,256]{0,1:T(8,128)(2,1)} %copy-done.35) | copy-start | bytes 786436
  572.4 38.8 %all-to-all-start.5 = ((bf16[16,128,256]{2,1,0:T(8,128)(2,1)}), bf16[16,128,256]{2,1,0:T(8,128)(2,1)}, u32[]{:S(2)}, u32[]{:S(2)}) async-start(bf16[16,128,256]{2,1,0:T(8,128)(2,1)} %bitcast.232), calls=%async_computation.8 | async-start | bytes 2097152 | tf_op jit(solution)/shard_map/all_to_all | solution.py:522
  581.5 142.0 %all-reduce.2.cloned.1.call-start = ((), (), s32[]{:S(2)}) async-start(), calls=%async_computation.15 | async-start | bytes 524288 | tf_op jit(solution)/shard_map/psum | solution.py:589
  588.2 142.1 %reduce-scatter.8.cloned.1.call-start = ((), (), s32[]{:S(2)}) async-start(), calls=%async_computation.14 | async-start | bytes 655360 | tf_op jit(solution)/shard_map/reduce_scatter | solution.py:602
  611.2 120.8 %copy-start.1 = (bf16[32,256,128]{2,1,0:T(8,128)(2,1)S(1)}, bf16[32,256,128]{2,1,0:T(8,128)(2,1)}, u32[]{:S(2)}) copy-start(bf16[32,256,128]{2,1,0:T(8,128)(2,1)} %param.17) | copy-start | bytes 6291460
  (40 other events, 136.2 us)
Sparse Core Ops, SparseCore 0:
  10.9 65.6 all-gather.16
  78.2 26.8 all-gather.10
  107.2 56.4 all-gather.18
  166.5 54.7 all-gather.20
  223.7 26.6 all-gather.12
  331.9 136.9 reduce-scatter.5
  472.5 59.5 all-gather.14
  534.4 146.5 reduce-scatter.3
  683.8 22.3 all-reduce.1
  708.6 21.6 reduce-scatter.7

commit v2 on v1

--- a/solution.py
+++ b/solution.py
@@ -392,27 +392,50 @@
     def cols_of(full_array, first_col, count):
         return lax.dynamic_slice_in_dim(full_array, first_col, count, 1)
 
-    def whole(block_array):
-        gathered = lax.all_gather(block_array, everyone, axis=0)
-        return from_blocks(gathered.reshape(token_blocks, row_size, tok_local, width_local))
-
-    inputs_f = whole(block_input).astype(jnp.float32)
+    def after(first, later):
+        return lax.optimization_barrier((first, later))[1]
+
+    def swap(blocks, names):
+        return lax.all_to_all(blocks, names, 0, 0, tiled=True)
+
+    def to_all(block_array, names, count):
+        return swap(jnp.broadcast_to(block_array, (count,) + block_array.shape), names)
+
+    def to_blocks_all(block_array):
+        sent_on = to_all(block_array, ("dp", "col"), token_blocks)
+        return sent_on.reshape(tokens, block_array.shape[1])
+
+    def summed(blocks, names):
+        return jnp.sum(swap(blocks, names).astype(jnp.float32), axis=0)
+
+    def block_sum(full_array):
+        blocks = full_array.reshape(token_blocks, tok_local, model_width)
+        return summed(blocks, ("dp", "col")).astype(jnp.bfloat16)
+
+    small = jnp.concatenate([w_router.T, attn_gain[None], ffn_gain[None]], axis=0)
+    small_all = to_all(small, "row", row_size).transpose(1, 0, 2).reshape(-1, model_width)
+    wide_input = to_all(block_input, "row", row_size).transpose(1, 0, 2)
+    inputs_all = to_blocks_all(wide_input.reshape(tok_local, model_width))
+    inputs_f = inputs_all.astype(jnp.float32)
     w_qkv_all = lax.all_gather(w_qkv, "row", axis=0, tiled=True)
-    small = jnp.concatenate([w_router, attn_gain[:, None], ffn_gain[:, None]], axis=1)
-    small_all = lax.all_gather(small, "row", axis=0, tiled=True)
-    w_router_all = small_all[:, :experts]
-    attn_gain_all = small_all[:, experts]
-    ffn_gain_all = small_all[:, experts + 1]
+    w_router_all = small_all[:experts].T
+    attn_gain_all = small_all[experts]
+    ffn_gain_all = small_all[experts + 1]
     routes_all = lax.all_gather(routes, "dp", axis=0, tiled=True)
     w_out_all = from_blocks(
-        lax.all_gather(w_out, ("col", "row"), axis=0).reshape(
+        lax.all_gather(after(w_qkv_all, w_out), ("col", "row"), axis=0).reshape(
             col_size, row_size, w_out.shape[0], width_local
         )
     )
-    grad_f = whole(out_grad).astype(jnp.float32)
+    grad_f = from_blocks(
+        lax.all_gather(after(w_out_all, out_grad), everyone, axis=0).reshape(
+            token_blocks, row_size, tok_local, width_local
+        )
+    ).astype(jnp.float32)
 
     def own_weight(weight):
         mine = lax.dynamic_slice_in_dim(weight, dp_index * owned, owned, 0)
+        mine = after(inputs_all, mine)
         moved = lax.all_to_all(mine, peers, 0, 0, tiled=True)
         return moved.reshape((row_size, col_size) + weight.shape[1:])
 
@@ -450,7 +473,7 @@
         .reshape(seq_len, head_cols)
     )
     attended_all = from_blocks(
-        lax.all_gather(attended, ("dp", "col"), axis=0).reshape(
+        to_all(attended, ("dp", "col"), token_blocks).reshape(
             dp_size, col_size, seq_len, head_cols
         )
     )
@@ -472,9 +495,9 @@
     sigmoid_gate = jax.nn.sigmoid(gate_pre)
     activated = (gate_pre * sigmoid_gate * up_val).astype(jnp.bfloat16)
     pair_out = jnp.dot(activated, down_own, preferred_element_type=jnp.float32)
-    gate_grads = lax.all_gather(
-        jnp.sum(grad_f * pair_out, axis=1), ("dp", "row", "col"), axis=0
-    ).T
+    gate_grads = to_all(
+        jnp.sum(grad_f * pair_out, axis=1).reshape(-1, 128), ("dp", "row", "col"), experts
+    ).reshape(experts, tokens).T
     gate_mix = gate_weights * (
         gate_grads - jnp.sum(gate_weights * gate_grads, axis=1, keepdims=True)
     )
@@ -491,20 +514,8 @@
     ) + lax.dot_general(
         up_grad, up_own, (((1,), (1,)), ((), ())), preferred_element_type=jnp.float32
     )
-    back_share = lax.psum_scatter(
-        token_back.astype(jnp.bfloat16), everyone, scatter_dimension=0, tiled=True
-    ).astype(jnp.float32)
-    moe_block = lax.psum_scatter(
-        to_blocks(
-            (gate_own_weight * pair_out).astype(jnp.bfloat16), tok_local, width_local
-        ).reshape(token_blocks * row_size, tok_local, width_local),
-        everyone,
-        scatter_dimension=0,
-        tiled=True,
-    ).reshape(tok_local, width_local)
-    own_hidden = cols_of(rows_of(hidden_res, block_first, tok_local), width_first, width_local)
-    block_output = (own_hidden + moe_block.astype(jnp.float32)).astype(jnp.bfloat16)
-
+    back_block = block_sum(token_back.astype(jnp.bfloat16))
+    back_share = summed(back_block.reshape(row_size, tok_share, model_width), "row")
     normed_grad = back_share + jnp.dot(
         rows_of(gate_mix, share_first, tok_share), w_router_all.T, precision=lax.Precision.HIGHEST
     )
@@ -514,12 +525,18 @@
     residual_share = rows_of(grad_f, share_first, tok_share) + rows_of(
         inv_rms_two, share_first, tok_share
     ) * (unit_grad_two - unit_share * jnp.mean(unit_grad_two * unit_share, axis=1, keepdims=True))
-    residual_all = lax.all_gather(
-        residual_share.astype(jnp.bfloat16), everyone, axis=0, tiled=True
-    )
+    residual_block = to_all(residual_share.astype(jnp.bfloat16), "row", row_size)
+    residual_all = to_blocks_all(residual_block.reshape(tok_local, model_width))
+
+    moe_block = block_sum(after(residual_all, (gate_own_weight * pair_out).astype(jnp.bfloat16)))
+    moe_own = summed(
+        moe_block.reshape(tok_local, row_size, width_local).transpose(1, 0, 2), "row"
+    )
+    own_hidden = cols_of(rows_of(hidden_res, block_first, tok_local), width_first, width_local)
+    block_output = (own_hidden + moe_own).astype(jnp.bfloat16)
 
     def expert_grad(blocks):
-        return lax.all_to_all(blocks, peers, 0, 0, tiled=True).astype(jnp.float32)
+        return swap(blocks, peers).astype(jnp.float32)
 
     def turned(left, right):
         return lax.dot_general(
@@ -586,9 +603,10 @@
         .reshape(seq_len, -1)
         .astype(jnp.bfloat16)
     )
-    grad_qkv = lax.psum(
-        turned(cols_of(normed_seq, width_first, width_local), qkv_grad).astype(jnp.bfloat16), "dp"
-    ).astype(jnp.float32)
+    qkv_part = turned(cols_of(normed_seq, width_first, width_local), qkv_grad)
+    grad_qkv = jnp.sum(
+        to_all(qkv_part.astype(jnp.bfloat16), "dp", dp_size).astype(jnp.float32), axis=0
+    )
     norm_back = lax.dot_general(
         qkv_grad, w_qkv, (((1,), (1,)), ((), ())), preferred_element_type=jnp.float32
     )
@@ -599,14 +617,20 @@
         norm_back * attn_gain - unit_own * (inner_part / model_width)
     )
     own_residual = cols_of(rows_of(residual_all, block_first, tok_local), width_first, width_local)
-    input_grad = own_residual.astype(jnp.float32) + lax.psum_scatter(
-        input_part, "col", scatter_dimension=0, tiled=True
+    input_grad = own_residual.astype(jnp.float32) + summed(
+        input_part.astype(jnp.bfloat16).reshape(col_size, tok_local, width_local), "col"
     )
     attn_gain_wide = lax.dynamic_update_slice_in_dim(
         jnp.zeros((model_width,), jnp.float32), attn_gain_part, width_first, 0
     )
-    gains = lax.psum(jnp.stack([attn_gain_wide, ffn_gain_part]), ("dp", "row", "col"))
-    gains_own = cols_of(gains, width_first, width_local)
+    gain_parts = jnp.stack([attn_gain_wide, ffn_gain_part]).reshape(2, row_size, width_local)
+    gains_own = summed(
+        jnp.broadcast_to(
+            gain_parts.transpose(1, 0, 2)[None, :, None],
+            (dp_size, row_size, col_size, 2, width_local),
+        ).reshape(experts, 2, width_local),
+        ("dp", "row", "col"),
+    )
     return (
         block_output,
         input_grad,

time: 748 us -> 558 us (0.75)
  waiting for transfers between devices: 393 us -> 223 us
  blocking collectives: 121 us -> 62.8 us
  starting transfers between devices: 37.1 us -> 80.2 us
  local copies, waits for them, and re-layouts: 65.3 us -> 51.5 us
    reduce_scatter x3 -> x0, waiting for transfers between devices: 207 us -> none  [the longest x1 135 us: expert_owner(): lax.psum_scatter(token_back.astype(jnp.bfloat16), everyone, scatter_dimen...]
    all_to_all x3 -> x14, waiting for transfers between devices: 28.8 us -> 143 us  [swap(): return lax.all_to_all(blocks, names, 0, 0, tiled=True)]
    all_gather x5 -> x2, waiting for transfers between devices: 102 us -> 23 us  [the longest x1 23 us: expert_owner(): lax.all_gather(after(w_out_all, out_grad), everyone, axis=0)]
    all_gather x2 -> x0, blocking collectives: 78.7 us -> none  [the longest x1 44 us: expert_owner(): lax.all_gather(jnp.sum(grad_f * pair_out, axis=1), ('dp', 'row', 'col'),...]
    all_to_all x0 -> x3, blocking collectives: none -> 57.9 us  [swap(): return lax.all_to_all(blocks, names, 0, 0, tiled=True)]
    all_to_all x3 -> x14, starting transfers between devices: 18 us -> 61.2 us  [swap(): return lax.all_to_all(blocks, names, 0, 0, tiled=True)]
    psum x1 -> x0, blocking collectives: 37.9 us -> none  [expert_owner(): lax.psum(jnp.stack([attn_gain_wide, ffn_gain_part]), ('dp', 'row', 'col'))]
    all_to_all x3, waiting for transfers between devices: 36.6 us -> 55.6 us  [own_weight(): moved = lax.all_to_all(mine, peers, 0, 0, tiled=True)]
  transfers between devices with their start and end apart: 16 -> 20, of which waited for: 12 -> 17; matrix products, arithmetic and copies ran while one was open for 17% -> 23% of each run, Pallas kernels for 0% -> 0%
where the time goes in v2:
time: 558 us; the launch traced here: 547 us
  waiting for transfers between devices  223 us (40%)
  starting transfers between devices  80.2 us (14%)
  matrix products  66.7 us (12%)
  blocking collectives  62.8 us (11%)
  local copies, waits for them, and re-layouts  51.5 us (9%)
  other arithmetic  48.2 us (9%)
  between operations  15.1 us (3%)
    all_to_all x14, waiting for transfers between devices, swap(): return lax.all_to_all(blocks, names, 0, 0, tiled=True)  143 us
    all_to_all x14, starting transfers between devices, swap(): return lax.all_to_all(blocks, names, 0, 0, tiled=True)  61.2 us
    all_to_all x3, blocking collectives, swap(): return lax.all_to_all(blocks, names, 0, 0, tiled=True)  57.9 us
    all_to_all x3, waiting for transfers between devices, own_weight(): moved = lax.all_to_all(mine, peers, 0, 0, tiled=True)  55.6 us
    all_gather x1, waiting for transfers between devices, expert_owner(): lax.all_gather(after(w_out_all, out_grad), everyone, axis=0)  23 us
    all_to_all x3, starting transfers between devices, own_weight(): moved = lax.all_to_all(mine, peers, 0, 0, tiled=True)  18.8 us
    dot_general x5, matrix products, turned(): lax.dot_general(left, right, (((0,), (0,)), ((), ())), preferred_element_...  13.2 us
    unnamed x91, local copies, waits for them, and re-layouts  11.7 us
  transfers between devices with their start and end apart: 20, of which 17 were waited for; matrix products, arithmetic and copies ran while one was open for 23% of the time, Pallas kernels for 0%

profile of v2, /device:TPU:0, one launch (start us, length us, event | category | flops | bytes accessed | tf_op | source)
XLA Modules:
  0.0 547.2 jit_solution(4531930197078770677)
XLA Ops:
  8.9 6.3 %all-to-all-start = ((bf16[4,128,256]{2,1,0:T(8,128)(2,1)}), bf16[4,128,256]{2,1,0:T(8,128)(2,1)S(1)}, u32[]{:S(2)}, u32[]{:S(2)}) async-start(bf16[4,128,256]{2,1,0:T(8,128)(2,1)} %broadcast_in_dim.86), calls=%async_computation | async-start | bytes 524288 | tf_op jit(solution)/shard_map/all_to_all | solution.py:399
  16.0 8.1 %all-to-all-done = bf16[4,128,256]{2,1,0:T(8,128)(2,1)S(1)} async-done(((bf16[4,128,256]{2,1,0:T(8,128)(2,1)}), bf16[4,128,256]{2,1,0:T(8,128)(2,1)S(1)}, u32[]{:S(2)}, u32[]{:S(2)}) %all-to-all-start) | async-done | bytes 262176 | tf_op jit(solution)/shard_map/all_to_all | solution.py:399
  28.5 5.6 %all-to-all-done.2 = f32[4,34,256]{2,1,0:T(8,128)S(1)} async-done(((f32[4,34,256]{2,1,0:T(8,128)}), f32[4,34,256]{2,1,0:T(8,128)S(1)}, u32[]{:S(2)}, u32[]{:S(2)}) %all-to-all-start.2) | async-done | bytes 139296 | tf_op jit(solution)/shard_map/all_to_all | solution.py:399
  42.0 24.7 %all-to-all-done.1 = bf16[8,128,1024]{2,1,0:T(8,128)(2,1)} async-done(((bf16[8,128,1024]{2,1,0:T(8,128)(2,1)}), bf16[8,128,1024]{2,1,0:T(8,128)(2,1)}, u32[]{:S(2)}, u32[]{:S(2)}) %all-to-all-start.1) | async-done | bytes 2097184 | tf_op jit(solution)/shard_map/all_to_all | solution.py:399
  69.4 4.8 convert_multiply_fusion
  91.4 25.5 %all-to-all-done.3 = bf16[8,512,256]{2,1,0:T(8,128)(2,1)} async-done(((bf16[8,512,256]{2,1,0:T(8,128)(2,1)}), bf16[8,512,256]{2,1,0:T(8,128)(2,1)}, u32[]{:S(2)}, u32[]{:S(2)}) %all-to-all-start.3) | async-done | bytes 2097184 | tf_op jit(solution)/shard_map/all_to_all | solution.py:399
  124.4 21.6 %all-to-all-done.4 = bf16[16,128,256]{2,1,0:T(8,128)(2,1)S(1)} async-done(((bf16[16,128,256]{2,1,0:T(8,128)(2,1)}), bf16[16,128,256]{2,1,0:T(8,128)(2,1)S(1)}, u32[]{:S(2)}, u32[]{:S(2)}) %all-to-all-start.4) | async-done | bytes 1048608 | tf_op jit(solution)/shard_map/all_to_all | solution.py:439
  146.0 8.3 %all-to-all-start.5 = ((bf16[16,256,128]{2,1,0:T(8,128)(2,1)}), bf16[16,256,128]{2,1,0:T(8,128)(2,1)S(1)}, u32[]{:S(2)}, u32[]{:S(2)}) async-start(bf16[16,256,128]{2,1,0:T(8,128)(2,1)} %get-tuple-element.19), calls=%async_computation.5 | async-start | bytes 2097152 | tf_op jit(solution)/shard_map/all_to_all | solution.py:439
  154.4 30.4 %all-to-all-done.5 = bf16[16,256,128]{2,1,0:T(8,128)(2,1)S(1)} async-done(((bf16[16,256,128]{2,1,0:T(8,128)(2,1)}), bf16[16,256,128]{2,1,0:T(8,128)(2,1)S(1)}, u32[]{:S(2)}, u32[]{:S(2)}) %all-to-all-start.5) | async-done | bytes 1048608 | tf_op jit(solution)/shard_map/all_to_all | solution.py:439
  184.8 6.8 %all-to-all-start.6 = ((bf16[16,256,128]{2,1,0:T(8,128)(2,1)}), bf16[16,256,128]{2,1,0:T(8,128)(2,1)}, u32[]{:S(2)}, u32[]{:S(2)}) async-start(bf16[16,256,128]{2,1,0:T(8,128)(2,1)} %get-tuple-element.20), calls=%async_computation.6 | async-start | bytes 2097152 | tf_op jit(solution)/shard_map/all_to_all | solution.py:439
  196.8 4.9 all_gather.23
  217.2 5.1 multiply_reduce_fusion.1
  232.6 23.0 %all-gather.10.cloned.1.call-done = bf16[4096,256]{1,0:T(8,128)(2,1)} async-done(((bf16[128,256]{1,0:T(8,128)(2,1)}), bf16[4096,256]{1,0:T(8,128)(2,1)}) %all-gather.10.cloned.1.call-update) | async-done | bytes 2097168 | tf_op jit(solution)/shard_map/all_gather | solution.py:431
  267.5 6.9 %fusion.97 = (f32[1024]{0:T(1024)S(1)}, f32[1024,32]{0,1:T(8,128)}) fusion(pred[1024,32]{0,1:T(8,128)(4,1)} %fusion.36, f32[1024,1024]{1,0:T(8,128)} %get-tuple-element.27, f32[32,1024]{1,0:T(8,128)S(1)} %bitcast.272), kind=kOutput, calls=%fused_computation.152 | convolution fusion | flops 402717696 | bytes 4493312 | tf_op jit(solution)/shard_map/dot_general | solution.py:485
  288.1 30.2 %all_to_all.100 = bf16[8,128,1024]{2,1,0:T(8,128)(2,1)S(1)} all-to-all(bf16[8,128,1024]{2,1,0:T(8,128)(2,1)S(1)} %bitcast.246), channel_id=1, replica_groups=mesh['dp'=2,'row'=4,'col'=4] {'dp','col'}, dimensions={0} | all-to-all | bytes 4194304 | tf_op jit(solution)/shard_map/all_to_all | solution.py:399
  341.0 18.2 %all-to-all-done.19 = bf16[16,128,256]{2,1,0:T(8,128)(2,1)S(1)} async-done(((bf16[16,128,256]{2,1,0:T(8,128)(2,1)}), bf16[16,128,256]{2,1,0:T(8,128)(2,1)S(1)}, u32[]{:S(2)}, u32[]{:S(2)}) %all-to-all-start.19) | async-done | bytes 1048608 | tf_op jit(solution)/shard_map/all_to_all | solution.py:399
  359.2 14.7 %all_to_all.101 = bf16[4,32,1024]{2,1,0:T(8,128)(2,1)S(1)} all-to-all(bf16[4,32,1024]{2,1,0:T(8,128)(2,1)S(1)} %broadcast_in_dim.96), channel_id=1, replica_groups=mesh['dp'=2,'row'=4,'col'=4] {'row'}, dimensions={0} | all-to-all | bytes 524288 | tf_op jit(solution)/shard_map/all_to_all | solution.py:399
  389.5 17.2 %all-to-all-done.11 = bf16[8,128,1024]{2,1,0:T(8,128)(2,1)} async-done(((bf16[8,128,1024]{2,1,0:T(8,128)(2,1)}), bf16[8,128,1024]{2,1,0:T(8,128)(2,1)}, u32[]{:S(2)}, u32[]{:S(2)}) %all-to-all-start.11) | async-done | bytes 2097184 | tf_op jit(solution)/shard_map/all_to_all | solution.py:399
  415.6 6.0 %fusion.3 = (f32[2,2,512]{2,1,0:T(2,128)}, f32[2,2,512,512]{2,3,1,0:T(8,128)}) fusion(f32[2,512,512,2]{2,1,3,0:T(8,128)} %fusion.79, pred[512,512]{0,1:T(8,128)(4,1)S(1)} %copy-done.34, bf16[512,2,64,1]{0,2,3,1:T(8,128)(2,1)S(1)} %copy-done.30, bf16[512,2,2,64]{0,3,2,1:T(8,128)(2,1)S(1)} %copy-done.21), kind=kOutput, calls=%fused_computation.8 | convolution fusion | flops 273678848 | bytes 9052160 | tf_op jit(solution)/shard_map/reduce_sum | solution.py:467
  428.4 5.5 %all-to-all-done.18 = bf16[16,256,128]{2,1,0:T(8,128)(2,1)} async-done(((bf16[16,256,128]{2,1,0:T(8,128)(2,1)}), bf16[16,256,128]{2,1,0:T(8,128)(2,1)}, u32[]{:S(2)}, u32[]{:S(2)}) %all-to-all-start.18) | async-done | bytes 1048608 | tf_op jit(solution)/shard_map/all_to_all | solution.py:399
  433.9 6.8 %all-to-all-start.17 = ((bf16[16,256,128]{2,1,0:T(8,128)(2,1)}), bf16[16,256,128]{2,1,0:T(8,128)(2,1)}, u32[]{:S(2)}, u32[]{:S(2)}) async-start(bf16[16,256,128]{2,1,0:T(8,128)(2,1)} %bitcast.257), calls=%async_computation.17 | async-start | bytes 2097152 | tf_op jit(solution)/shard_map/all_to_all | solution.py:399
  450.8 12.8 %all-to-all-done.17 = bf16[16,256,128]{2,1,0:T(8,128)(2,1)} async-done(((bf16[16,256,128]{2,1,0:T(8,128)(2,1)}), bf16[16,256,128]{2,1,0:T(8,128)(2,1)}, u32[]{:S(2)}, u32[]{:S(2)}) %all-to-all-start.17) | async-done | bytes 1048608 | tf_op jit(solution)/shard_map/all_to_all | solution.py:399
  463.7 13.0 %all_to_all.102 = f32[32,2,256]{2,1,0:T(2,128)S(1)} all-to-all(f32[32,2,256]{2,1,0:T(2,128)S(1)} %bitcast.285), channel_id=1, replica_groups=mesh['dp'=2,'row'=4,'col'=4] {'dp','row','col'}, dimensions={0} | all-to-all | bytes 131072 | tf_op jit(solution)/shard_map/all_to_all | solution.py:399
  501.9 15.6 %all-to-all-done.12 = bf16[8,128,1024]{2,1,0:T(8,128)(2,1)} async-done(((bf16[8,128,1024]{2,1,0:T(8,128)(2,1)}), bf16[8,128,1024]{2,1,0:T(8,128)(2,1)}, u32[]{:S(2)}, u32[]{:S(2)}) %all-to-all-start.12) | async-done | bytes 2097184 | tf_op jit(solution)/shard_map/all_to_all | solution.py:399
  (219 shorter events, 210.0 us)
Async XLA Ops:
  7.2 83.1 %copy-start = (bf16[32,128,256]{2,1,0:T(8,128)(2,1)S(1)}, bf16[32,128,256]{2,1,0:T(8,128)(2,1)}, u32[]{:S(2)}) copy-start(bf16[32,128,256]{2,1,0:T(8,128)(2,1)} %param.19) | copy-start | bytes 6291460
  8.9 15.3 %all-to-all-start = ((bf16[4,128,256]{2,1,0:T(8,128)(2,1)}), bf16[4,128,256]{2,1,0:T(8,128)(2,1)S(1)}, u32[]{:S(2)}, u32[]{:S(2)}) async-start(bf16[4,128,256]{2,1,0:T(8,128)(2,1)} %broadcast_in_dim.86), calls=%async_computation | async-start | bytes 524288 | tf_op jit(solution)/shard_map/all_to_all | solution.py:399
  24.8 9.3 %all-to-all-start.2 = ((f32[4,34,256]{2,1,0:T(8,128)}), f32[4,34,256]{2,1,0:T(8,128)S(1)}, u32[]{:S(2)}, u32[]{:S(2)}) async-start(f32[4,34,256]{2,1,0:T(8,128)} %broadcast_in_dim.90), calls=%async_computation.2 | async-start | bytes 327680 | tf_op jit(solution)/shard_map/all_to_all | solution.py:399
  35.7 31.0 %all-to-all-start.1 = ((bf16[8,128,1024]{2,1,0:T(8,128)(2,1)}), bf16[8,128,1024]{2,1,0:T(8,128)(2,1)}, u32[]{:S(2)}, u32[]{:S(2)}) async-start(bf16[8,128,1024]{2,1,0:T(8,128)(2,1)} %broadcast_in_dim.87), calls=%async_computation.1 | async-start | bytes 4194304 | tf_op jit(solution)/shard_map/all_to_all | solution.py:399
  40.1 34.1 %all-gather.6.cloned.1.call-start = ((), (), s32[]{:S(2)}) async-start(), calls=%async_computation.20 | async-start | bytes 1310720 | tf_op jit(solution)/shard_map/all_gather | solution.py:420
  85.9 31.0 %all-to-all-start.3 = ((bf16[8,512,256]{2,1,0:T(8,128)(2,1)}), bf16[8,512,256]{2,1,0:T(8,128)(2,1)}, u32[]{:S(2)}, u32[]{:S(2)}) async-start(bf16[8,512,256]{2,1,0:T(8,128)(2,1)} %broadcast_in_dim.93), calls=%async_computation.3 | async-start | bytes 4194304 | tf_op jit(solution)/shard_map/all_to_all | solution.py:399
  116.9 29.1 %all-to-all-start.4 = ((bf16[16,128,256]{2,1,0:T(8,128)(2,1)}), bf16[16,128,256]{2,1,0:T(8,128)(2,1)S(1)}, u32[]{:S(2)}, u32[]{:S(2)}) async-start(bf16[16,128,256]{2,1,0:T(8,128)(2,1)} %constant_dynamic-slice_fusion.3), calls=%async_computation.4 | async-start | bytes 2097152 | tf_op jit(solution)/shard_map/all_to_all | solution.py:439
  120.6 71.2 %all-gather.8.cloned.1.call-start = ((), (), s32[]{:S(2)}) async-start(), calls=%async_computation.21 | async-start | bytes 2228224 | tf_op jit(solution)/shard_map/all_gather | solution.py:426
  146.0 38.8 %copy-start.9 = (bf16[16,128,256]{2,1,0:T(8,128)(2,1)}, bf16[16,128,256]{2,1,0:T(8,128)(2,1)S(1)}, u32[]{:S(2)}) copy-start(bf16[16,128,256]{2,1,0:T(8,128)(2,1)S(1)} %all-to-all-done.4) | copy-start | bytes 3145732
  146.0 38.8 %all-to-all-start.5 = ((bf16[16,256,128]{2,1,0:T(8,128)(2,1)}), bf16[16,256,128]{2,1,0:T(8,128)(2,1)S(1)}, u32[]{:S(2)}, u32[]{:S(2)}) async-start(bf16[16,256,128]{2,1,0:T(8,128)(2,1)} %get-tuple-element.19), calls=%async_computation.5 | async-start | bytes 2097152 | tf_op jit(solution)/shard_map/all_to_all | solution.py:439
  184.8 30.2 %all-to-all-start.6 = ((bf16[16,256,128]{2,1,0:T(8,128)(2,1)}), bf16[16,256,128]{2,1,0:T(8,128)(2,1)}, u32[]{:S(2)}, u32[]{:S(2)}) async-start(bf16[16,256,128]{2,1,0:T(8,128)(2,1)} %get-tuple-element.20), calls=%async_computation.6 | async-start | bytes 2097152 | tf_op jit(solution)/shard_map/all_to_all | solution.py:439
  191.6 63.9 %all-gather.10.cloned.1.call-start = ((), (), s32[]{:S(2)}) async-start(), calls=%async_computation.22 | async-start | bytes 2162688 | tf_op jit(solution)/shard_map/all_gather | solution.py:431
  209.5 50.5 %copy-start.7 = (bf16[64,8,4,256]{3,1,2,0:T(8,128)(2,1)}, bf16[64,8,4,256]{3,1,2,0:T(8,128)(2,1)S(1)}, u32[]{:S(2)}) copy-start(bf16[64,8,4,256]{3,1,2,0:T(8,128)(2,1)S(1)} %copy.218) | copy-start | bytes 3145732
  263.9 13.5 %all-to-all-start.9 = ((f32[32,8,128]{2,1,0:T(8,128)}), f32[32,8,128]{2,1,0:T(8,128)}, u32[]{:S(2)}, u32[]{:S(2)}) async-start(f32[32,8,128]{2,1,0:T(8,128)} %broadcast_in_dim.95), calls=%async_computation.9 | async-start | bytes 262144 | tf_op jit(solution)/shard_map/all_to_all | solution.py:399
  319.4 13.1 %all-to-all-start.8 = ((bf16[4,32,1024]{2,1,0:T(8,128)(2,1)}), bf16[4,32,1024]{2,1,0:T(8,128)(2,1)}, u32[]{:S(2)}, u32[]{:S(2)}) async-start(bf16[4,32,1024]{2,1,0:T(8,128)(2,1)} %bitcast.274), calls=%async_computation.8 | async-start | bytes 524288 | tf_op jit(solution)/shard_map/all_to_all | solution.py:399
  332.5 26.7 %all-to-all-start.19 = ((bf16[16,128,256]{2,1,0:T(8,128)(2,1)}), bf16[16,128,256]{2,1,0:T(8,128)(2,1)S(1)}, u32[]{:S(2)}, u32[]{:S(2)}) async-start(bf16[16,128,256]{2,1,0:T(8,128)(2,1)} %bitcast.75), calls=%async_computation.19 | async-start | bytes 2097152 | tf_op jit(solution)/shard_map/all_to_all | solution.py:399
  337.4 21.8 %copy-start.24 = (f32[1024,32]{0,1:T(8,128)}, f32[1024,32]{0,1:T(8,128)S(1)}, u32[]{:S(2)}) copy-start(f32[1024,32]{0,1:T(8,128)S(1)} %fusion.62) | copy-start | bytes 393220
  375.5 31.2 %all-to-all-start.11 = ((bf16[8,128,1024]{2,1,0:T(8,128)(2,1)}), bf16[8,128,1024]{2,1,0:T(8,128)(2,1)}, u32[]{:S(2)}, u32[]{:S(2)}) async-start(bf16[8,128,1024]{2,1,0:T(8,128)(2,1)} %broadcast_in_dim.97), calls=%async_computation.11 | async-start | bytes 4194304 | tf_op jit(solution)/shard_map/all_to_all | solution.py:399
  406.7 27.2 %all-to-all-start.18 = ((bf16[16,256,128]{2,1,0:T(8,128)(2,1)}), bf16[16,256,128]{2,1,0:T(8,128)(2,1)}, u32[]{:S(2)}, u32[]{:S(2)}) async-start(bf16[16,256,128]{2,1,0:T(8,128)(2,1)} %bitcast.73), calls=%async_computation.18 | async-start | bytes 2097152 | tf_op jit(solution)/shard_map/all_to_all | solution.py:399
  433.9 29.7 %all-to-all-start.17 = ((bf16[16,256,128]{2,1,0:T(8,128)(2,1)}), bf16[16,256,128]{2,1,0:T(8,128)(2,1)}, u32[]{:S(2)}, u32[]{:S(2)}) async-start(bf16[16,256,128]{2,1,0:T(8,128)(2,1)} %bitcast.257), calls=%async_computation.17 | async-start | bytes 2097152 | tf_op jit(solution)/shard_map/all_to_all | solution.py:399
  476.7 9.4 %all-to-all-start.14 = ((bf16[4,128,256]{2,1,0:T(8,128)(2,1)}), bf16[4,128,256]{2,1,0:T(8,128)(2,1)S(1)}, u32[]{:S(2)}, u32[]{:S(2)}) async-start(bf16[4,128,256]{2,1,0:T(8,128)(2,1)} %bitcast.62), calls=%async_computation.14 | async-start | bytes 524288 | tf_op jit(solution)/shard_map/all_to_all | solution.py:399
  486.1 31.4 %all-to-all-start.12 = ((bf16[8,128,1024]{2,1,0:T(8,128)(2,1)}), bf16[8,128,1024]{2,1,0:T(8,128)(2,1)}, u32[]{:S(2)}, u32[]{:S(2)}) async-start(bf16[8,128,1024]{2,1,0:T(8,128)(2,1)} %bitcast.42), calls=%async_computation.12 | async-start | bytes 4194304 | tf_op jit(solution)/shard_map/all_to_all | solution.py:399
  518.3 10.1 %all-to-all-start.16 = ((bf16[2,256,512]{2,1,0:T(8,128)(2,1)}), bf16[2,256,512]{2,1,0:T(8,128)(2,1)S(1)}, u32[]{:S(2)}, u32[]{:S(2)}) async-start(bf16[2,256,512]{2,1,0:T(8,128)(2,1)} %broadcast_in_dim.102), calls=%async_computation.16 | async-start | bytes 1048576 | tf_op jit(solution)/shard_map/all_to_all | solution.py:399
  528.3 10.2 %all-to-all-start.13 = ((bf16[4,128,256]{2,1,0:T(8,128)(2,1)}), bf16[4,128,256]{2,1,0:T(8,128)(2,1)S(1)}, u32[]{:S(2)}, u32[]{:S(2)}) async-start(bf16[4,128,256]{2,1,0:T(8,128)(2,1)} %copy.191), calls=%async_computation.13 | async-start | bytes 524288 | tf_op jit(solution)/shard_map/all_to_all | solution.py:399
  (39 other events, 152.7 us)
Sparse Core Ops, SparseCore 0:
  42.5 27.7 all-gather.5
  123.6 56.1 all-gather.7
  196.9 58.5 all-gather.9

commit v3 on v2

--- a/solution.py
+++ b/solution.py
@@ -435,7 +435,6 @@
 
     def own_weight(weight):
         mine = lax.dynamic_slice_in_dim(weight, dp_index * owned, owned, 0)
-        mine = after(inputs_all, mine)
         moved = lax.all_to_all(mine, peers, 0, 0, tiled=True)
         return moved.reshape((row_size, col_size) + weight.shape[1:])
 

time: 558 us -> 539 us (0.966)
  waiting for transfers between devices: 223 us -> 190 us
  blocking collectives: 62.8 us -> 86.8 us
  starting transfers between devices: 80.2 us -> 72.7 us
    all_to_all x14 -> x13, waiting for transfers between devices: 143 us -> 109 us  [swap(): return lax.all_to_all(blocks, names, 0, 0, tiled=True)]
    all_to_all x3 -> x4, blocking collectives: 57.9 us -> 71.1 us  [swap(): return lax.all_to_all(blocks, names, 0, 0, tiled=True)]
    all_gather x1, blocking collectives: 4.87 us -> 15.7 us  [expert_owner(): routes_all = lax.all_gather(routes, 'dp', axis=0, tiled=True)]
    all_to_all x14 -> x13, starting transfers between devices: 61.2 us -> 55 us  [swap(): return lax.all_to_all(blocks, names, 0, 0, tiled=True)]
    all_to_all x3, waiting for transfers between devices: 55.6 us -> 61.7 us  [own_weight(): moved = lax.all_to_all(mine, peers, 0, 0, tiled=True)]
    unnamed x91 -> x93, local copies, waits for them, and re-layouts: 11.7 us -> 13.6 us
  transfers between devices with their start and end apart: 20 -> 19, of which waited for: 17 -> 16; matrix products, arithmetic and copies ran while one was open for 23% -> 25% of each run, Pallas kernels for 0% -> 0%
where the time goes in v3:
time: 539 us; the launch traced here: 528 us
  waiting for transfers between devices  190 us (35%)
  blocking collectives  86.8 us (16%)
  starting transfers between devices  72.7 us (13%)
  matrix products  62.2 us (12%)
  local copies, waits for them, and re-layouts  57 us (11%)
  other arithmetic  44.2 us (8%)
  between operations  15.1 us (3%)
    all_to_all x13, waiting for transfers between devices, swap(): return lax.all_to_all(blocks, names, 0, 0, tiled=True)  109 us
    all_to_all x4, blocking collectives, swap(): return lax.all_to_all(blocks, names, 0, 0, tiled=True)  71.1 us
    all_to_all x3, waiting for transfers between devices, own_weight(): moved = lax.all_to_all(mine, peers, 0, 0, tiled=True)  61.7 us
    all_to_all x13, starting transfers between devices, swap(): return lax.all_to_all(blocks, names, 0, 0, tiled=True)  55 us
    all_gather x1, waiting for transfers between devices, expert_owner(): lax.all_gather(after(w_out_all, out_grad), everyone, axis=0)  17.8 us
    all_to_all x3, starting transfers between devices, own_weight(): moved = lax.all_to_all(mine, peers, 0, 0, tiled=True)  17.6 us
    all_gather x1, blocking collectives, expert_owner(): routes_all = lax.all_gather(routes, 'dp', axis=0, tiled=True)  15.7 us
    unnamed x93, local copies, waits for them, and re-layouts  13.6 us
  transfers between devices with their start and end apart: 19, of which 16 were waited for; matrix products, arithmetic and copies ran while one was open for 25% of the time, Pallas kernels for 0%

profile of v3, /device:TPU:0, one launch (start us, length us, event | category | flops | bytes accessed | tf_op | source)
XLA Modules:
  0.0 528.0 jit_solution(10823244588479246146)
XLA Ops:
  8.2 13.2 %all_to_all.100 = f32[4,34,256]{2,1,0:T(8,128)} all-to-all(f32[4,34,256]{2,1,0:T(8,128)S(1)} %broadcast_in_dim.90), channel_id=1, replica_groups=mesh['dp'=2,'row'=4,'col'=4] {'row'}, dimensions={0} | all-to-all | bytes 278528 | tf_op jit(solution)/shard_map/all_to_all | solution.py:399
  27.4 6.9 %all-to-all-done = bf16[4,128,256]{2,1,0:T(8,128)(2,1)S(1)} async-done(((bf16[4,128,256]{2,1,0:T(8,128)(2,1)}), bf16[4,128,256]{2,1,0:T(8,128)(2,1)S(1)}, u32[]{:S(2)}, u32[]{:S(2)}) %all-to-all-start) | async-done | bytes 262176 | tf_op jit(solution)/shard_map/all_to_all | solution.py:399
  38.3 22.5 %all-to-all-done.6 = bf16[16,256,128]{2,1,0:T(8,128)(2,1)S(1)} async-done(((bf16[16,256,128]{2,1,0:T(8,128)(2,1)}), bf16[16,256,128]{2,1,0:T(8,128)(2,1)S(1)}, u32[]{:S(2)}, u32[]{:S(2)}) %all-to-all-start.6) | async-done | bytes 1048608 | tf_op jit(solution)/shard_map/all_to_all | solution.py:438
  70.0 23.6 %all-to-all-done.1 = bf16[8,128,1024]{2,1,0:T(8,128)(2,1)S(1)} async-done(((bf16[8,128,1024]{2,1,0:T(8,128)(2,1)}), bf16[8,128,1024]{2,1,0:T(8,128)(2,1)S(1)}, u32[]{:S(2)}, u32[]{:S(2)}) %all-to-all-start.1) | async-done | bytes 2097184 | tf_op jit(solution)/shard_map/all_to_all | solution.py:399
  93.6 5.5 %all-to-all-start.5 = ((bf16[16,256,128]{2,1,0:T(8,128)(2,1)}), bf16[16,256,128]{2,1,0:T(8,128)(2,1)S(1)}, u32[]{:S(2)}, u32[]{:S(2)}) async-start(bf16[16,256,128]{2,1,0:T(8,128)(2,1)} %constant_dynamic-slice_fusion.2), calls=%async_computation.5 | async-start | bytes 2097152 | tf_op jit(solution)/shard_map/all_to_all | solution.py:438
  105.2 19.4 %all-to-all-done.5 = bf16[16,256,128]{2,1,0:T(8,128)(2,1)S(1)} async-done(((bf16[16,256,128]{2,1,0:T(8,128)(2,1)}), bf16[16,256,128]{2,1,0:T(8,128)(2,1)S(1)}, u32[]{:S(2)}, u32[]{:S(2)}) %all-to-all-start.5) | async-done | bytes 1048608 | tf_op jit(solution)/shard_map/all_to_all | solution.py:438
  124.6 8.4 %all-to-all-start.4 = ((bf16[16,128,256]{2,1,0:T(8,128)(2,1)}), bf16[16,128,256]{2,1,0:T(8,128)(2,1)}, u32[]{:S(2)}, u32[]{:S(2)}) async-start(bf16[16,128,256]{2,1,0:T(8,128)(2,1)} %constant_dynamic-slice_fusion.3), calls=%async_computation.4 | async-start | bytes 2097152 | tf_op jit(solution)/shard_map/all_to_all | solution.py:438
  143.8 19.7 %all-to-all-done.4 = bf16[16,128,256]{2,1,0:T(8,128)(2,1)} async-done(((bf16[16,128,256]{2,1,0:T(8,128)(2,1)}), bf16[16,128,256]{2,1,0:T(8,128)(2,1)}, u32[]{:S(2)}, u32[]{:S(2)}) %all-to-all-start.4) | async-done | bytes 1048608 | tf_op jit(solution)/shard_map/all_to_all | solution.py:438
  175.5 15.7 %all_gather.23 = s32[1024,8]{0,1:T(8,128)S(1)} all-gather(s32[512,8]{0,1:T(8,128)S(1)} %copy-done.36), channel_id=1, replica_groups=mesh['dp'=2,'row'=4,'col'=4] {'dp'}, dimensions={0}, use_global_device_ids=true | all-gather | bytes 49152 | tf_op jit(solution)/shard_map/all_gather | solution.py:424
  218.7 17.8 %all-gather.10.cloned.1.call-done = bf16[4096,256]{1,0:T(8,128)(2,1)} async-done(((bf16[128,256]{1,0:T(8,128)(2,1)}), bf16[4096,256]{1,0:T(8,128)(2,1)}) %all-gather.10.cloned.1.call-update) | async-done | bytes 2097168 | tf_op jit(solution)/shard_map/all_gather | solution.py:431
  248.4 6.9 %fusion.98 = (f32[1024]{0:T(1024)S(1)}, f32[1024,32]{0,1:T(8,128)}) fusion(pred[1024,32]{0,1:T(8,128)(4,1)} %fusion.37, f32[1024,1024]{1,0:T(8,128)} %get-tuple-element.21, f32[32,1024]{1,0:T(8,128)S(1)} %bitcast.273), kind=kOutput, calls=%fused_computation.153 | convolution fusion | flops 402717696 | bytes 4493312 | tf_op jit(solution)/shard_map/dot_general | solution.py:484
  269.0 30.2 %all_to_all.101 = bf16[8,128,1024]{2,1,0:T(8,128)(2,1)S(1)} all-to-all(bf16[8,128,1024]{2,1,0:T(8,128)(2,1)S(1)} %bitcast.247), channel_id=1, replica_groups=mesh['dp'=2,'row'=4,'col'=4] {'dp','col'}, dimensions={0} | all-to-all | bytes 4194304 | tf_op jit(solution)/shard_map/all_to_all | solution.py:399
  300.3 4.6 all-to-all-start.8
  321.9 18.2 %all-to-all-done.19 = bf16[16,128,256]{2,1,0:T(8,128)(2,1)S(1)} async-done(((bf16[16,128,256]{2,1,0:T(8,128)(2,1)}), bf16[16,128,256]{2,1,0:T(8,128)(2,1)S(1)}, u32[]{:S(2)}, u32[]{:S(2)}) %all-to-all-start.19) | async-done | bytes 1048608 | tf_op jit(solution)/shard_map/all_to_all | solution.py:399
  340.1 14.7 %all_to_all.102 = bf16[4,32,1024]{2,1,0:T(8,128)(2,1)S(1)} all-to-all(bf16[4,32,1024]{2,1,0:T(8,128)(2,1)S(1)} %broadcast_in_dim.96), channel_id=1, replica_groups=mesh['dp'=2,'row'=4,'col'=4] {'row'}, dimensions={0} | all-to-all | bytes 524288 | tf_op jit(solution)/shard_map/all_to_all | solution.py:399
  370.4 17.2 %all-to-all-done.11 = bf16[8,128,1024]{2,1,0:T(8,128)(2,1)} async-done(((bf16[8,128,1024]{2,1,0:T(8,128)(2,1)}), bf16[8,128,1024]{2,1,0:T(8,128)(2,1)}, u32[]{:S(2)}, u32[]{:S(2)}) %all-to-all-start.11) | async-done | bytes 2097184 | tf_op jit(solution)/shard_map/all_to_all | solution.py:399
  396.5 6.0 %fusion.3 = (f32[2,2,512]{2,1,0:T(2,128)}, f32[2,2,512,512]{2,3,1,0:T(8,128)}) fusion(f32[2,512,512,2]{2,1,3,0:T(8,128)} %fusion.80, pred[512,512]{0,1:T(8,128)(4,1)S(1)} %copy-done.34, bf16[512,2,64,1]{0,2,3,1:T(8,128)(2,1)S(1)} %copy-done.30, bf16[512,2,2,64]{0,3,2,1:T(8,128)(2,1)S(1)} %copy-done.22), kind=kOutput, calls=%fused_computation.6 | convolution fusion | flops 273678848 | bytes 9052160 | tf_op jit(solution)/shard_map/reduce_sum | solution.py:466
  402.5 4.6 fusion.5
  409.3 5.5 %all-to-all-done.18 = bf16[16,256,128]{2,1,0:T(8,128)(2,1)} async-done(((bf16[16,256,128]{2,1,0:T(8,128)(2,1)}), bf16[16,256,128]{2,1,0:T(8,128)(2,1)}, u32[]{:S(2)}, u32[]{:S(2)}) %all-to-all-start.18) | async-done | bytes 1048608 | tf_op jit(solution)/shard_map/all_to_all | solution.py:399
  414.8 6.8 %all-to-all-start.17 = ((bf16[16,256,128]{2,1,0:T(8,128)(2,1)}), bf16[16,256,128]{2,1,0:T(8,128)(2,1)}, u32[]{:S(2)}, u32[]{:S(2)}) async-start(bf16[16,256,128]{2,1,0:T(8,128)(2,1)} %bitcast.260), calls=%async_computation.17 | async-start | bytes 2097152 | tf_op jit(solution)/shard_map/all_to_all | solution.py:399
  431.7 12.8 %all-to-all-done.17 = bf16[16,256,128]{2,1,0:T(8,128)(2,1)} async-done(((bf16[16,256,128]{2,1,0:T(8,128)(2,1)}), bf16[16,256,128]{2,1,0:T(8,128)(2,1)}, u32[]{:S(2)}, u32[]{:S(2)}) %all-to-all-start.17) | async-done | bytes 1048608 | tf_op jit(solution)/shard_map/all_to_all | solution.py:399
  444.6 13.0 %all_to_all.103 = f32[32,2,256]{2,1,0:T(2,128)S(1)} all-to-all(f32[32,2,256]{2,1,0:T(2,128)S(1)} %bitcast.286), channel_id=1, replica_groups=mesh['dp'=2,'row'=4,'col'=4] {'dp','row','col'}, dimensions={0} | all-to-all | bytes 131072 | tf_op jit(solution)/shard_map/all_to_all | solution.py:399
  466.9 4.7 all-to-all-start.12
  482.7 15.6 %all-to-all-done.12 = bf16[8,128,1024]{2,1,0:T(8,128)(2,1)} async-done(((bf16[8,128,1024]{2,1,0:T(8,128)(2,1)}), bf16[8,128,1024]{2,1,0:T(8,128)(2,1)}, u32[]{:S(2)}, u32[]{:S(2)}) %all-to-all-start.12) | async-done | bytes 2097184 | tf_op jit(solution)/shard_map/all_to_all | solution.py:399
  (221 shorter events, 199.4 us)
Async XLA Ops:
  7.2 19.2 %copy-start = (bf16[32,256,128]{2,1,0:T(8,128)(2,1)S(1)}, bf16[32,256,128]{2,1,0:T(8,128)(2,1)}, u32[]{:S(2)}) copy-start(bf16[32,256,128]{2,1,0:T(8,128)(2,1)} %param.17) | copy-start | bytes 6291460
  22.9 11.4 %all-to-all-start = ((bf16[4,128,256]{2,1,0:T(8,128)(2,1)}), bf16[4,128,256]{2,1,0:T(8,128)(2,1)S(1)}, u32[]{:S(2)}, u32[]{:S(2)}) async-start(bf16[4,128,256]{2,1,0:T(8,128)(2,1)} %broadcast_in_dim.86), calls=%async_computation | async-start | bytes 524288 | tf_op jit(solution)/shard_map/all_to_all | solution.py:399
  34.3 26.5 %all-to-all-start.6 = ((bf16[16,256,128]{2,1,0:T(8,128)(2,1)}), bf16[16,256,128]{2,1,0:T(8,128)(2,1)S(1)}, u32[]{:S(2)}, u32[]{:S(2)}) async-start(bf16[16,256,128]{2,1,0:T(8,128)(2,1)} %constant_dynamic-slice_fusion.1), calls=%async_computation.6 | async-start | bytes 2097152 | tf_op jit(solution)/shard_map/all_to_all | solution.py:438
  62.5 31.1 %all-to-all-start.1 = ((bf16[8,128,1024]{2,1,0:T(8,128)(2,1)}), bf16[8,128,1024]{2,1,0:T(8,128)(2,1)S(1)}, u32[]{:S(2)}, u32[]{:S(2)}) async-start(bf16[8,128,1024]{2,1,0:T(8,128)(2,1)} %broadcast_in_dim.87), calls=%async_computation.1 | async-start | bytes 4194304 | tf_op jit(solution)/shard_map/all_to_all | solution.py:399
  67.0 32.6 %all-gather.6.cloned.1.call-start = ((), (), s32[]{:S(2)}) async-start(), calls=%async_computation.20 | async-start | bytes 1310720 | tf_op jit(solution)/shard_map/all_gather | solution.py:420
  93.6 31.0 %all-to-all-start.5 = ((bf16[16,256,128]{2,1,0:T(8,128)(2,1)}), bf16[16,256,128]{2,1,0:T(8,128)(2,1)S(1)}, u32[]{:S(2)}, u32[]{:S(2)}) async-start(bf16[16,256,128]{2,1,0:T(8,128)(2,1)} %constant_dynamic-slice_fusion.2), calls=%async_computation.5 | async-start | bytes 2097152 | tf_op jit(solution)/shard_map/all_to_all | solution.py:438
  99.1 71.3 %all-gather.8.cloned.1.call-start = ((), (), s32[]{:S(2)}) async-start(), calls=%async_computation.21 | async-start | bytes 2228224 | tf_op jit(solution)/shard_map/all_gather | solution.py:426
  124.6 39.0 %all-to-all-start.4 = ((bf16[16,128,256]{2,1,0:T(8,128)(2,1)}), bf16[16,128,256]{2,1,0:T(8,128)(2,1)}, u32[]{:S(2)}, u32[]{:S(2)}) async-start(bf16[16,128,256]{2,1,0:T(8,128)(2,1)} %constant_dynamic-slice_fusion.3), calls=%async_computation.4 | async-start | bytes 2097152 | tf_op jit(solution)/shard_map/all_to_all | solution.py:438
  166.0 35.0 %all-to-all-start.3 = ((bf16[8,512,256]{2,1,0:T(8,128)(2,1)}), bf16[8,512,256]{2,1,0:T(8,128)(2,1)}, u32[]{:S(2)}, u32[]{:S(2)}) async-start(bf16[8,512,256]{2,1,0:T(8,128)(2,1)} %broadcast_in_dim.93), calls=%async_computation.3 | async-start | bytes 4194304 | tf_op jit(solution)/shard_map/all_to_all | solution.py:399
  170.3 66.1 %all-gather.10.cloned.1.call-start = ((), (), s32[]{:S(2)}) async-start(), calls=%async_computation.22 | async-start | bytes 2162688 | tf_op jit(solution)/shard_map/all_gather | solution.py:431
  175.5 20.5 %copy-start.11 = (bf16[16,256,128]{2,1,0:T(8,128)(2,1)S(1)}, bf16[16,256,128]{2,1,0:T(8,128)(2,1)}, u32[]{:S(2)}) copy-start(bf16[16,256,128]{2,1,0:T(8,128)(2,1)} %copy-done.10) | copy-start | bytes 3145732
  218.7 22.2 %copy-start.19 = (bf16[1024,512]{1,0:T(8,128)(2,1)}, bf16[1024,512]{1,0:T(8,128)(2,1)S(1)}, u32[]{:S(2)}) copy-start(bf16[1024,512]{1,0:T(8,128)(2,1)S(1)} %get-tuple-element.47) | copy-start | bytes 3145732
  244.8 13.4 %all-to-all-start.9 = ((f32[32,8,128]{2,1,0:T(8,128)}), f32[32,8,128]{2,1,0:T(8,128)}, u32[]{:S(2)}, u32[]{:S(2)}) async-start(f32[32,8,128]{2,1,0:T(8,128)} %broadcast_in_dim.95), calls=%async_computation.9 | async-start | bytes 262144 | tf_op jit(solution)/shard_map/all_to_all | solution.py:399
  300.3 13.1 %all-to-all-start.8 = ((bf16[4,32,1024]{2,1,0:T(8,128)(2,1)}), bf16[4,32,1024]{2,1,0:T(8,128)(2,1)}, u32[]{:S(2)}, u32[]{:S(2)}) async-start(bf16[4,32,1024]{2,1,0:T(8,128)(2,1)} %bitcast.275), calls=%async_computation.8 | async-start | bytes 524288 | tf_op jit(solution)/shard_map/all_to_all | solution.py:399
  313.4 26.7 %all-to-all-start.19 = ((bf16[16,128,256]{2,1,0:T(8,128)(2,1)}), bf16[16,128,256]{2,1,0:T(8,128)(2,1)S(1)}, u32[]{:S(2)}, u32[]{:S(2)}) async-start(bf16[16,128,256]{2,1,0:T(8,128)(2,1)} %bitcast.75), calls=%async_computation.19 | async-start | bytes 2097152 | tf_op jit(solution)/shard_map/all_to_all | solution.py:399
  318.3 21.8 %copy-start.25 = (f32[1024,32]{0,1:T(8,128)}, f32[1024,32]{0,1:T(8,128)S(1)}, u32[]{:S(2)}) copy-start(f32[1024,32]{0,1:T(8,128)S(1)} %fusion.63) | copy-start | bytes 393220
  340.1 16.3 %copy-start.5 = (bf16[16,128,256]{2,1,0:T(8,128)(2,1)}, bf16[16,128,256]{2,1,0:T(8,128)(2,1)S(1)}, u32[]{:S(2)}) copy-start(bf16[16,128,256]{2,1,0:T(8,128)(2,1)S(1)} %all-to-all-done.19) | copy-start | bytes 3145732
  356.4 31.1 %all-to-all-start.11 = ((bf16[8,128,1024]{2,1,0:T(8,128)(2,1)}), bf16[8,128,1024]{2,1,0:T(8,128)(2,1)}, u32[]{:S(2)}, u32[]{:S(2)}) async-start(bf16[8,128,1024]{2,1,0:T(8,128)(2,1)} %broadcast_in_dim.97), calls=%async_computation.11 | async-start | bytes 4194304 | tf_op jit(solution)/shard_map/all_to_all | solution.py:399
  387.6 27.2 %all-to-all-start.18 = ((bf16[16,256,128]{2,1,0:T(8,128)(2,1)}), bf16[16,256,128]{2,1,0:T(8,128)(2,1)}, u32[]{:S(2)}, u32[]{:S(2)}) async-start(bf16[16,256,128]{2,1,0:T(8,128)(2,1)} %bitcast.73), calls=%async_computation.18 | async-start | bytes 2097152 | tf_op jit(solution)/shard_map/all_to_all | solution.py:399
  414.8 29.7 %all-to-all-start.17 = ((bf16[16,256,128]{2,1,0:T(8,128)(2,1)}), bf16[16,256,128]{2,1,0:T(8,128)(2,1)}, u32[]{:S(2)}, u32[]{:S(2)}) async-start(bf16[16,256,128]{2,1,0:T(8,128)(2,1)} %bitcast.260), calls=%async_computation.17 | async-start | bytes 2097152 | tf_op jit(solution)/shard_map/all_to_all | solution.py:399
  457.5 9.4 %all-to-all-start.14 = ((bf16[4,128,256]{2,1,0:T(8,128)(2,1)}), bf16[4,128,256]{2,1,0:T(8,128)(2,1)S(1)}, u32[]{:S(2)}, u32[]{:S(2)}) async-start(bf16[4,128,256]{2,1,0:T(8,128)(2,1)} %bitcast.62), calls=%async_computation.14 | async-start | bytes 524288 | tf_op jit(solution)/shard_map/all_to_all | solution.py:399
  466.9 31.4 %all-to-all-start.12 = ((bf16[8,128,1024]{2,1,0:T(8,128)(2,1)}), bf16[8,128,1024]{2,1,0:T(8,128)(2,1)}, u32[]{:S(2)}, u32[]{:S(2)}) async-start(bf16[8,128,1024]{2,1,0:T(8,128)(2,1)} %bitcast.42), calls=%async_computation.12 | async-start | bytes 4194304 | tf_op jit(solution)/shard_map/all_to_all | solution.py:399
  499.1 10.1 %all-to-all-start.16 = ((bf16[2,256,512]{2,1,0:T(8,128)(2,1)}), bf16[2,256,512]{2,1,0:T(8,128)(2,1)S(1)}, u32[]{:S(2)}, u32[]{:S(2)}) async-start(bf16[2,256,512]{2,1,0:T(8,128)(2,1)} %broadcast_in_dim.102), calls=%async_computation.16 | async-start | bytes 1048576 | tf_op jit(solution)/shard_map/all_to_all | solution.py:399
  509.2 10.2 %all-to-all-start.13 = ((bf16[4,128,256]{2,1,0:T(8,128)(2,1)}), bf16[4,128,256]{2,1,0:T(8,128)(2,1)S(1)}, u32[]{:S(2)}, u32[]{:S(2)}) async-start(bf16[4,128,256]{2,1,0:T(8,128)(2,1)} %copy.191), calls=%async_computation.13 | async-start | bytes 524288 | tf_op jit(solution)/shard_map/all_to_all | solution.py:399
  (39 other events, 133.9 us)
Sparse Core Ops, SparseCore 0:
  69.3 30.1 all-gather.5
  102.1 56.9 all-gather.7
  175.6 60.8 all-gather.9
